TPU v7x, 128 devices: a whole 4x4x4 slice. The times are simulated.
128 devices in a mesh: ctx: 32 (over x, z, core), tp: 4 (over y).
Axes of the slice: x: 4, y: 4, z: 4, core: 2. Of those that a mesh axis runs over, the one named last changes fastest.
Arguments:
- normed_input: bfloat16 [16384, 4096], P('ctx'), may hold values from -12 to 12
- w_query: bfloat16 [4096, 2048], P(None, 'tp'), may hold values from -0.09375 to 0.09375
- key_weight: bfloat16 [4096, 512], P(None, 'tp'), may hold values from -0.09375 to 0.09375
- value_weight: bfloat16 [4096, 512], P(None, 'tp'), may hold values from -0.09375 to 0.09375
- output_weight: bfloat16 [4096, 2048], P(None, 'tp'), may hold values from -0.125 to 0.125
- output_cotangent: bfloat16 [16384, 4096], P('ctx'), may hold values from -6 to 6
- piece_doc: int32 [2048], replicated, may hold values from 0 to 127, as said below
- piece_offset: int32 [2048], replicated, may hold values from 0 to 480, as said below
- doc_owner: int32 [128], replicated, may hold values from 0 to 31, as said below
Outputs:
- grad_in: bfloat16 [16384, 4096], P('ctx', 'tp')
- grad_query: bfloat16 [4096, 2048], P('ctx', 'tp')
- grad_key: bfloat16 [4096, 512], P('ctx', 'tp')
- grad_value: bfloat16 [4096, 512], P('ctx', 'tp')
- grad_out: bfloat16 [4096, 2048], P('ctx', 'tp')
Inputs may be any that keep to these rules, and one draw needn't show every extreme that they name: `piece_doc`: every document has at least one piece; the pieces of one document, in increasing token order, have offsets 0, 8, 16 and so on. `piece_offset`: A piece belongs to the owner of its document. The pieces of the tokens of one index of ctx go to exactly 32 / 2 owners, exactly 32 tokens to each of them; so every owner receives 512 tokens. `doc_owner`: every device of ctx owns exactly 4 documents.
All inputs are finite; a program needn't handle non-finite values.
Results may differ from a plain program's by a relative error of at most 0.015.
Values may be sent and summed in bfloat16 or wider, within the bound.
No kernel may reach another device: no remote copies, remote signals or barrier semaphores. Data moves between devices by JAX's collectives and lax.ppermute only.
A program may use at most 128 MiB of HBM per device.

v0:
```python
import functools
import math

import jax
import jax.numpy as jnp
import numpy as np
from jax import lax
from jax.experimental import pallas as pl
from jax.experimental.pallas import tpu as pltpu
from jax.sharding import Mesh, PartitionSpec as P


HEAD = 128
PIECE = 8
ROPE_BASE = 500000.0
FILL = -1e30
NX, NZ, NC, NT = 4, 4, 2, 4
CTX = ("x", "z", "c")
N_CTX = NX * NZ * NC
TOK = 512
WIDTH = 4096
QW = 512
KW = 128
COLS = 1280
K0, V0, G0 = 512, 640, 768
PAIR = 32
TARGETS = 16
PIECES = TOK // PIECE
MAX_POS = 512
HALF = 640
CUT = HALF // 2
FAR, UP, OWN, DOWN = 0, 1, 2, 3
SCALE = 1.0 / math.sqrt(HEAD)
BF = jnp.bfloat16
F32 = jnp.float32
I32 = jnp.int32
NN = (((1,), (0,)), ((), ()))
NTD = (((1,), (1,)), ((), ()))
TN = (((0,), (0,)), ((), ()))
TOKEN = jax.ShapeDtypeStruct((8, HEAD), F32)
TOKEN_SPEC = pl.BlockSpec((8, HEAD), lambda *_: (0, 0))


def dot(a, b, dims=NN):
    return lax.dot_general(a, b, dims, preferred_element_type=F32)


def vmem_spec():
    return pl.BlockSpec(memory_space=pltpu.VMEM)


def smem_spec():
    return pl.BlockSpec(memory_space=pltpu.SMEM)


def any_spec():
    return pl.BlockSpec(memory_space=pl.ANY)


def params(mib):
    return pltpu.CompilerParams(vmem_limit_bytes=mib * 1024 * 1024)


def cost(flops, nbytes):
    return pl.CostEstimate(flops=int(flops), bytes_accessed=int(nbytes), transcendentals=0)


def rotary_tables():
    half = HEAD // 2
    frequency = np.float32(ROPE_BASE) ** (-2.0 * np.arange(half, dtype=np.float32) / np.float32(HEAD))
    angles = np.arange(MAX_POS, dtype=np.float32)[:, None] * frequency.astype(np.float32)[None, :]
    cosine, sine = np.cos(angles), np.sin(angles)
    return (
        jnp.asarray(np.concatenate([cosine, cosine], axis=1).astype(np.float32)),
        jnp.asarray(np.concatenate([-sine, sine], axis=1).astype(np.float32)),
    )


def related(coordinate, order):
    return (coordinate + 2 - order) & 3


def store_blocks(rows, target, which, sems):
    copies = [
        pltpu.make_async_copy(rows.at[pl.ds(k * PAIR, PAIR)], target.at[which[k]], sems.at[k])
        for k in range(TARGETS)
    ]
    for copy in copies:
        copy.start()
    return copies


def project_kernel(
    me,
    piece_doc,
    piece_offset,
    doc_owner,
    x_hbm,
    c_hbm,
    wq_hbm,
    wk_hbm,
    wv_hbm,
    wo_hbm,
    cos_table,
    sin_table,
    out_ref,
    token,
    x_ref,
    c_ref,
    wq_ref,
    wkv_ref,
    wo_ref,
    made,
    packed,
    final,
    slot_of,
    count,
    first,
    targets,
    load_sems,
    sems,
):
    span = 2 * HEAD
    copy = pltpu.make_async_copy
    token[...] = jnp.zeros_like(token)
    get_x = copy(x_hbm, x_ref, load_sems.at[0])
    get_k = copy(wk_hbm, wkv_ref.at[:, pl.ds(0, KW)], load_sems.at[1])
    get_v = copy(wv_hbm, wkv_ref.at[:, pl.ds(KW, KW)], load_sems.at[2])
    get_c = copy(c_hbm, c_ref, load_sems.at[3])

    def part(i, source, into, sem):
        at = pl.ds(pl.multiple_of(i * span, span), span)
        return copy(source.at[:, at], into.at[i], load_sems.at[sem + i])

    get_x.start()
    get_k.start()
    get_v.start()
    for i in range(2):
        part(i, wq_hbm, wq_ref, 4).start()
    get_c.start()
    for i in range(2):
        part(i, wo_hbm, wo_ref, 6).start()

    for o in range(N_CTX):
        count[o] = 0
    for i in range(PIECES):
        owner = doc_owner[piece_doc[me[0] * PIECES + i]]
        slot_of[i] = owner * PIECES + count[owner]
        count[owner] = count[owner] + 1
    run = jnp.int32(0)
    for o in range(N_CTX):
        first[o] = run
        targets[run >> 2] = jnp.int32(o)
        run = run + count[o]
    for i in range(PIECES):
        key = slot_of[i]
        slot_of[i] = (first[key >> 6] + (key & (PIECES - 1))) * PIECE

    def pack(base, rotated):
        for i in range(PIECES):
            to = pl.multiple_of(slot_of[i], PIECE)
            here = slice(i * PIECE, (i + 1) * PIECE)
            if rotated:
                at = pl.multiple_of(piece_offset[me[0] * PIECES + i], PIECE)
                cosine = cos_table[pl.ds(at, PIECE), :]
                sine = sin_table[pl.ds(at, PIECE), :]
            for h in range(2):
                u = made[here, h * HEAD : (h + 1) * HEAD]
                if h < rotated:
                    u = u * cosine + pltpu.roll(u, HEAD // 2, 1) * sine
                packed[pl.ds(to, PIECE), h * HEAD : (h + 1) * HEAD] = u
        final[:, pl.ds(base, span)] = packed[...].astype(BF)

    get_x.wait()
    get_k.wait()
    get_v.wait()
    made[...] = dot(x_ref[...], wkv_ref[...])
    pack(K0, 1)

    @pl.loop(0, 2)
    def _(i):
        part(i, wq_hbm, wq_ref, 4).wait()
        made[...] = dot(x_ref[...], wq_ref[i])
        pack(pl.multiple_of(i * span, span), 2)

    get_c.wait()

    @pl.loop(0, 2)
    def _(i):
        part(i, wo_hbm, wo_ref, 6).wait()
        made[...] = dot(c_ref[...], wo_ref[i])
        pack(pl.multiple_of(G0 + i * span, span), 0)

    for each in store_blocks(final, out_ref, targets, sems):
        each.wait()


def project(me, piece_doc, piece_offset, doc_owner, x, c, wq, wk, wv, wo, cos_table, sin_table):
    span = 2 * HEAD
    smem = pltpu.SMEM
    return pl.pallas_call(
        project_kernel,
        in_specs=[smem_spec()] * 4 + [any_spec()] * 6 + [vmem_spec()] * 2,
        out_specs=[any_spec(), vmem_spec()],
        scratch_shapes=[
            pltpu.VMEM((TOK, WIDTH), BF),
            pltpu.VMEM((TOK, WIDTH), BF),
            pltpu.VMEM((2, WIDTH, span), BF),
            pltpu.VMEM((WIDTH, 2 * KW), BF),
            pltpu.VMEM((2, WIDTH, span), BF),
            pltpu.VMEM((TOK, span), F32),
            pltpu.VMEM((TOK, span), F32),
            pltpu.VMEM((TOK, COLS), BF),
            smem((PIECES,), I32),
            smem((N_CTX,), I32),
            smem((N_CTX,), I32),
            smem((N_CTX,), I32),
            pltpu.SemaphoreType.DMA((8,)),
            pltpu.SemaphoreType.DMA((TARGETS,)),
        ],
        out_shape=[jax.ShapeDtypeStruct((N_CTX, PAIR, COLS), BF), TOKEN],
        compiler_params=params(60),
        cost_estimate=cost(6e9, 24e6),
        name="project",
    )(me, piece_doc, piece_offset, doc_owner, x, c, wq, wk, wv, wo, cos_table, sin_table)


def regroup_kernel(where, after, x_ref, c_ref, xk_ref, xs_ref, ck_ref, cs_ref, token):
    token[...] = jnp.zeros_like(token)
    core = where[2]
    for i in range(NZ):
        base = related(where[1], i) * 2
        keep = pl.ds(pl.multiple_of((base + core) * HEAD, HEAD), HEAD)
        send = pl.ds(pl.multiple_of((base + 1 - core) * HEAD, HEAD), HEAD)
        xk_ref[i] = x_ref[:, keep]
        xs_ref[i] = x_ref[:, send]
        ck_ref[i] = c_ref[:, keep]
        cs_ref[i] = c_ref[:, send]


def regroup(where, after, x, c):
    part = pl.BlockSpec((TOK, WIDTH // NX), lambda i, where: (0, related(where[0], i)))
    half = jax.ShapeDtypeStruct((NX * NZ, TOK, HEAD), BF)
    return pl.pallas_call(
        regroup_kernel,
        grid_spec=pltpu.PrefetchScalarGridSpec(
            num_scalar_prefetch=1,
            grid=(NX,),
            in_specs=[any_spec(), part, part],
            out_specs=[pl.BlockSpec((NZ, TOK, HEAD), lambda i, where: (i, 0, 0))] * 4 + [TOKEN_SPEC],
        ),
        out_shape=[half] * 4 + [TOKEN],
        compiler_params=params(16),
        cost_estimate=cost(1, 17e6),
        name="regroup",
    )(where, after, x, c)


def fetch_blocks(source, which, rows, sems):
    copies = [
        pltpu.make_async_copy(source.at[which[k]], rows.at[pl.ds(k * PAIR, PAIR)], sems.at[k])
        for k in range(TARGETS)
    ]
    for copy in copies:
        copy.start()
    return copies


def attend_kernel(
    live,
    offsets,
    got_ref,
    cos_table,
    sin_table,
    doc_col,
    doc_row,
    pos_col,
    pos_row,
    token_x,
    token_f,
    token_r,
    out_ref,
    rows,
    back,
    bias,
    cos_rows,
    sin_rows,
    sems,
):
    copies = fetch_blocks(got_ref, live, rows, sems)
    for i in range(PIECES):
        at = pl.multiple_of(offsets[i], PIECE)
        cos_rows[i * PIECE : (i + 1) * PIECE, :] = cos_table[pl.ds(at, PIECE), :]
        sin_rows[i * PIECE : (i + 1) * PIECE, :] = sin_table[pl.ds(at, PIECE), :]
    allowed = (doc_col[...] == doc_row[...]) & (pos_row[...] <= pos_col[...])
    bias[...] = jnp.where(allowed, 0.0, FILL)
    for copy in copies:
        copy.wait()
    keys = rows[:, K0:V0]
    values = rows[:, V0:G0]
    key_grad = jnp.zeros((TOK, HEAD), F32)
    value_grad = jnp.zeros((TOK, HEAD), F32)
    half = HEAD // 2

    def unrotate(u):
        return u * cos_rows[...] - pltpu.roll(u, half, 1) * sin_rows[...]

    for h in range(QW // HEAD):
        here = slice(h * HEAD, (h + 1) * HEAD)
        there = slice(G0 + h * HEAD, G0 + (h + 1) * HEAD)
        query = rows[:, here]
        grads = rows[:, there]
        scores = dot(query, keys, NTD) * SCALE + bias[...]
        weight = jnp.exp(scores - jnp.max(scores, axis=1, keepdims=True))
        prob = weight * (1.0 / jnp.sum(weight, axis=1, keepdims=True))
        rounded = prob.astype(BF)
        attended = dot(rounded, values).astype(BF)
        back[:, there] = attended
        delta = jnp.sum(grads.astype(F32) * attended.astype(F32), axis=1, keepdims=True)
        prob_grad = dot(grads, values, NTD)
        score_grad = (prob * (prob_grad - delta)).astype(BF)
        back[:, here] = unrotate(dot(score_grad, keys) * SCALE).astype(BF)
        key_grad = key_grad + dot(score_grad, query, TN)
        value_grad = value_grad + dot(rounded, grads, TN)
    back[:, K0:V0] = unrotate(key_grad * SCALE).astype(BF)
    back[:, V0:G0] = value_grad.astype(BF)
    for k in range(TARGETS):
        out_ref[live[k]] = back[k * PAIR : (k + 1) * PAIR, :]


def attend(live, offsets, got, cos_table, sin_table, doc_col, doc_row, pos_col, pos_row, *tokens):
    return pl.pallas_call(
        attend_kernel,
        in_specs=[smem_spec(), smem_spec(), any_spec()] + [vmem_spec()] * 6 + [any_spec()] * 3,
        out_specs=vmem_spec(),
        out_shape=jax.ShapeDtypeStruct((N_CTX, PAIR, COLS), BF),
        scratch_shapes=[
            pltpu.VMEM((TOK, COLS), BF),
            pltpu.VMEM((TOK, COLS), BF),
            pltpu.VMEM((TOK, TOK), F32),
            pltpu.VMEM((TOK, HEAD), F32),
            pltpu.VMEM((TOK, HEAD), F32),
            pltpu.SemaphoreType.DMA((TARGETS,)),
        ],
        compiler_params=params(28),
        cost_estimate=cost(4e9, 6e6),
        name="attend",
    )(live, offsets, got, cos_table, sin_table, doc_col, doc_row, pos_col, pos_row, *tokens)


def stage_kernel(where, after, wq_ref, wk_ref, wv_ref, out_ref, token):
    token[...] = jnp.zeros_like(token)
    out_ref[:, :K0] = wq_ref[...]
    out_ref[:, K0:V0] = wk_ref[...]
    out_ref[:, V0:] = wv_ref[...]


def stage_weights(where, after, at, count, wq, wk, wv):
    span = WIDTH // NT
    block = lambda i, where: (related(where[3], at + i), 0)
    return pl.pallas_call(
        stage_kernel,
        grid_spec=pltpu.PrefetchScalarGridSpec(
            num_scalar_prefetch=1,
            grid=(count,),
            in_specs=[
                any_spec(),
                pl.BlockSpec((span, QW), block),
                pl.BlockSpec((span, KW), block),
                pl.BlockSpec((span, KW), block),
            ],
            out_specs=[pl.BlockSpec((span, G0), lambda i, *_: (i, 0)), TOKEN_SPEC],
        ),
        out_shape=[jax.ShapeDtypeStruct((count * span, G0), BF), TOKEN],
        compiler_params=params(12),
        cost_estimate=cost(1, 3e6 * count),
        name="stage_weights",
    )(where, after, wq, wk, wv)


def restore_kernel(targets, got_ref, rows_ref, out_ref, packed, sems):
    copies = fetch_blocks(got_ref, targets, packed, sems)
    slot = lax.broadcasted_iota(I32, (TOK, TOK), 0)
    one_hot = jnp.where(slot == rows_ref[...], 1.0, 0.0).astype(BF)
    for copy in copies:
        copy.wait()
    out_ref[...] = dot(one_hot, packed[...], TN).astype(BF)


def restore(targets, got, rows):
    return pl.pallas_call(
        restore_kernel,
        in_specs=[smem_spec(), any_spec(), vmem_spec()],
        out_specs=vmem_spec(),
        out_shape=jax.ShapeDtypeStruct((TOK, COLS), BF),
        scratch_shapes=[pltpu.VMEM((TOK, COLS), BF), pltpu.SemaphoreType.DMA((TARGETS,))],
        compiler_params=params(16),
        cost_estimate=cost(0.7e9, 4e6),
        name="restore",
    )(targets, got, rows)


def input_grad_kernel(after, dy_ref, w_ref, *outs):
    total = dot(dy_ref[:, :G0], w_ref[...], NTD).astype(BF)
    if len(outs) == 1:
        outs[0][...] = total
    else:
        outs[0][...] = total[: TOK // 2]
        outs[1][...] = total[TOK // 2 :]


def input_grad(after, at, count, dy, weights, split=False):
    span = WIDTH // NT
    if split:
        out_shape = [jax.ShapeDtypeStruct((TOK // 2, span), BF)] * 2
        out_specs = [pl.BlockSpec((TOK // 2, span), lambda i: (0, 0))] * 2
    else:
        out_shape = jax.ShapeDtypeStruct((count * TOK, span), BF)
        out_specs = pl.BlockSpec((TOK, span), lambda i: (i, 0))
    return pl.pallas_call(
        input_grad_kernel,
        grid=(count,),
        in_specs=[
            any_spec(),
            pl.BlockSpec((TOK, COLS), lambda i: (0, 0)),
            pl.BlockSpec((span, G0), lambda i: (at + 2 * i, 0)),
        ],
        out_specs=out_specs,
        out_shape=out_shape,
        compiler_params=params(20),
        cost_estimate=cost(0.8e9 * count, 5e6 * count),
        name="input_grad",
    )(after, dy, weights)


def weight_grad_kernel(after, own, peer, xa0, xa1, c0, c1, b00, b01, b02, b03, b10, b11, b12, b13, *outs):
    wide = lambda ref: jnp.concatenate([ref[j] for j in range(NZ)], axis=1)
    join = lambda refs: jnp.concatenate([ref[0] for ref in refs], axis=1)
    first = dot(own[:, V0:G0], wide(xa0), TN) + dot(peer[:, V0:G0], wide(xa1), TN)
    second = dot(own[:, G0:], wide(c0), TN) + dot(peer[:, G0:], wide(c1), TN)
    third = dot(own[:, :V0], join([b00, b01, b02, b03]), TN) + dot(
        peer[:, :V0], join([b10, b11, b12, b13]), TN
    )
    if len(outs) == 4:
        a0, a1, b0, b1 = outs
        a0[:KW, :] = first.astype(BF)
        a0[KW:, :] = second[: CUT - KW].astype(BF)
        a1[...] = second[CUT - KW :].astype(BF)
        b0[...] = third[:CUT].astype(BF)
        b1[...] = third[CUT:].astype(BF)
    else:
        a, b = outs
        a[:KW, :] = first.astype(BF)
        a[KW:, :] = second.astype(BF)
        b[...] = third.astype(BF)


def weight_grad(after, at, count, split, own, peer, xk, xr, ck, cr):
    wide = NZ * HEAD
    whole = lambda i: (0, 0)
    spec_a = pl.BlockSpec((NZ, TOK, HEAD), lambda i: (at + 2 * i, 0, 0))
    specs_b = [
        pl.BlockSpec((1, TOK, HEAD), functools.partial(lambda j, i: (j * NZ + at + 2 * i, 0, 0), j))
        for j in range(NX)
    ]
    if split:
        out_shape = [jax.ShapeDtypeStruct((CUT, wide), BF)] * 4
        out_specs = [pl.BlockSpec((CUT, wide), whole)] * 4
    else:
        out_shape = [jax.ShapeDtypeStruct((count * HALF, wide), BF)] * 2
        out_specs = [pl.BlockSpec((HALF, wide), lambda i: (i, 0))] * 2
    return pl.pallas_call(
        weight_grad_kernel,
        grid=(count,),
        in_specs=[any_spec(), pl.BlockSpec((TOK, COLS), whole), pl.BlockSpec((TOK, COLS), whole)]
        + [spec_a] * 4
        + specs_b
        + specs_b,
        out_specs=out_specs,
        out_shape=out_shape,
        compiler_params=params(28),
        cost_estimate=cost(1.4e9 * count, 6e6 * count),
        name="weight_grad",
    )(after, own, peer, xk, xr, ck, cr, xk, xk, xk, xk, xr, xr, xr, xr)


def near_kernel(count, *refs):
    for g in range(count):
        near, below, above = refs[3 * g : 3 * g + 3]
        up, down = refs[3 * count + 2 * g : 3 * count + 2 * g + 2]
        rows = up.shape[0]
        cut = rows // 2
        up[:cut] = (near[:cut].astype(F32) + below[...].astype(F32)).astype(BF)
        up[cut:] = near[cut:rows]
        down[:cut] = near[rows : rows + cut]
        down[cut:] = (near[rows + cut :].astype(F32) + above[...].astype(F32)).astype(BF)


def add_near(*groups):
    flat = [value for group in groups for value in group]
    shapes = []
    for near, _, _ in groups:
        shapes += [jax.ShapeDtypeStruct((near.shape[0] // 2, near.shape[1]), BF)] * 2
    return pl.pallas_call(
        functools.partial(near_kernel, len(groups)),
        in_specs=[vmem_spec()] * len(flat),
        out_specs=[vmem_spec()] * len(shapes),
        out_shape=shapes,
        compiler_params=params(16),
        cost_estimate=cost(1e6, 5e6),
        name="add_near",
    )(*flat)


def total_kernel(own_a, up_a, down_a, own_b, up_b, down_b, *outs):
    for g, (own, up, down) in enumerate(((own_a, up_a, down_a), (own_b, up_b, down_b))):
        total = own[...].astype(F32) + up[...].astype(F32) + down[...].astype(F32)
        for place in range(NZ):
            ref = outs[4 * g + place]
            ref[...] = total[:, place * HEAD : (place + 1) * HEAD].astype(ref.dtype)


def add_total(own_a, near_a, own_b, near_b):
    one = [jax.ShapeDtypeStruct((HALF, HEAD), F32 if place == OWN else BF) for place in range(NZ)]
    return pl.pallas_call(
        total_kernel,
        in_specs=[vmem_spec()] * 6,
        out_specs=[vmem_spec()] * 8,
        out_shape=one + one,
        compiler_params=params(16),
        cost_estimate=cost(1e6, 5e6),
        name="add_total",
    )(own_a, *near_a, own_b, *near_b)


def finish_kernel(*refs):
    ins, (query, key, value, out) = refs[:8], refs[8:]
    a, b = (sum(ref[...].astype(F32) for ref in ins[4 * g : 4 * g + 4]).T for g in range(2))
    value[...] = a[:, :KW].astype(BF)
    out[...] = a[:, KW:].astype(BF)
    query[...] = b[:, :QW].astype(BF)
    key[...] = b[:, QW:].astype(BF)


def finish(own_a, got_a, own_b, got_b):
    shape = lambda n: jax.ShapeDtypeStruct((HEAD, n), BF)
    return pl.pallas_call(
        finish_kernel,
        in_specs=[vmem_spec()] * 8,
        out_specs=[vmem_spec()] * 4,
        out_shape=[shape(QW), shape(KW), shape(KW), shape(QW)],
        compiler_params=params(16),
        cost_estimate=cost(1e6, 2e6),
        name="finish",
    )(own_a, *got_a, own_b, *got_b)


def shift(value, axis, by):
    n = lax.axis_size(axis)
    return lax.ppermute(value, axis, [(i, (i + by) % n) for i in range(n)])


def both_ways(up, down, axis):
    return shift(up, axis, 1), shift(down, axis, -1)


def all_ways(parts, axis):
    return shift(parts[FAR], axis, 2), shift(parts[UP], axis, 1), shift(parts[DOWN], axis, -1)


def on_device(x, wq, wk, wv, wo, c, piece_doc, piece_offset, doc_owner):
    ix, iz, ic, iy = (lax.axis_index(a) for a in ("x", "z", "c", "tp"))
    me = (ix * NZ + iz) * NC + ic
    cos_table, sin_table = rotary_tables()
    sent, token_p = project(
        me.reshape(1), piece_doc, piece_offset, doc_owner, x, c, wq, wk, wv, wo, cos_table, sin_table
    )
    got = lax.all_to_all(sent, CTX, split_axis=0, concat_axis=0, tiled=True)
    where = jnp.stack([ix, iz, ic, iy]).astype(I32)
    xk, xs, ck, cs, token_x = regroup(where, token_p, x, c)
    w_far, token_f = stage_weights(where, token_p, FAR, 1, wq, wk, wv)
    w_rest, token_r = stage_weights(where, token_p, UP, 3, wq, wk, wv)
    xr = shift(xs, "c", 1)
    cr = shift(cs, "c", 1)

    doc_grid = piece_doc.reshape(N_CTX, PIECES)
    own_doc = lax.dynamic_slice_in_dim(piece_doc, me * PIECES, PIECES)
    doc_ids = jnp.arange(doc_owner.shape[0], dtype=I32)
    own_owner = jnp.sum(jnp.where(own_doc[:, None] == doc_ids[None, :], doc_owner[None, :], 0), axis=1)
    ids = jnp.arange(PIECES, dtype=I32)
    order_key = own_owner * PIECES + ids
    slot = jnp.sum((order_key[None, :] < order_key[:, None]).astype(I32), axis=1)
    blocks = jnp.arange(TARGETS, dtype=I32) * (PAIR // PIECE)
    targets = jnp.sum(jnp.where(blocks[:, None] == slot[None, :], own_owner[None, :], 0), axis=1)
    within = jnp.arange(PIECE, dtype=I32)
    packed_row = (slot[:, None] * PIECE + within[None, :]).reshape(1, TOK)

    mine_doc = doc_owner == me
    doc_rank = jnp.sum((mine_doc[None, :] & (doc_ids[None, :] < doc_ids[:, None])).astype(I32), axis=1)
    four = jnp.arange(4, dtype=I32)
    my_docs = jnp.sum(
        jnp.where(mine_doc[None, :] & (doc_rank[None, :] == four[:, None]), doc_ids[None, :], 0), axis=1
    )
    mine = jnp.any(doc_grid[None, :, :] == my_docs[:, None, None], axis=0)
    before = (ids[:, None] < ids[None, :]).astype(BF)
    rank_in = jnp.dot(mine.astype(BF), before, preferred_element_type=F32).astype(I32)
    is_live = jnp.any(mine, axis=1)
    sources = jnp.arange(N_CTX, dtype=I32)
    live_rank = jnp.sum((is_live[None, :] & (sources[None, :] < sources[:, None])).astype(I32), axis=1)
    kth = jnp.arange(TARGETS, dtype=I32)
    live = jnp.sum(
        jnp.where(is_live[None, :] & (live_rank[None, :] == kth[:, None]), sources[None, :], 0), axis=1
    )
    index = jnp.where(mine, live_rank[:, None] * (PAIR // PIECE) + rank_in, -1).reshape(1, -1)
    chosen = index == ids[:, None]
    live_doc = jnp.sum(jnp.where(chosen, piece_doc[None, :], 0), axis=1)
    live_offset = jnp.sum(jnp.where(chosen, piece_offset[None, :], 0), axis=1)
    row_doc = jnp.repeat(live_doc, PIECE)
    row_pos = (live_offset[:, None] + within[None, :]).reshape(-1)

    back = attend(
        live,
        live_offset,
        got,
        cos_table,
        sin_table,
        row_doc[:, None],
        row_doc[None, :],
        row_pos[:, None],
        row_pos[None, :],
        token_x,
        token_f,
        token_r,
    )
    home = lax.all_to_all(back, CTX, split_axis=0, concat_axis=0, tiled=True)
    dy = restore(targets, home, packed_row)
    peer = shift(dy, "c", 1)
    y0, y1 = input_grad(dy, 0, 1, dy, w_far, split=True)
    a0, a1, b0, b1 = weight_grad(y0, FAR, 1, True, dy, peer, xk, xr, ck, cr)
    y0, y1, a0, a1, b0, b1 = lax.optimization_barrier((y0, y1, a0, a1, b0, b1))
    a_far = both_ways(a0, a1, "x")
    b_far = both_ways(b0, b1, "z")
    y_far = both_ways(y0, y1, "tp")
    a_near, b_near = weight_grad(a0, UP, 2, False, dy, peer, xk, xr, ck, cr)
    sums = add_near((a_near, *a_far), (b_near, *b_far))
    a_got = both_ways(*sums[:2], "x")
    b_got = both_ways(*sums[2:], "z")
    y_near = input_grad(sums[0], UP - 1, 2, dy, w_rest)
    y_sums = add_near((y_near, *y_far))
    y_got = both_ways(*y_sums, "tp")
    a_own, b_own = weight_grad(y_near, OWN, 1, False, dy, peer, xk, xr, ck, cr)
    y_own = input_grad(a_own, OWN - 1, 1, dy, w_rest)
    parts = add_total(a_own, a_got, b_own, b_got)
    a_got = all_ways(parts[:4], "z")
    b_got = all_ways(parts[4:], "x")
    grad_in = (
        y_own.astype(F32) + y_got[0].astype(F32) + y_got[1].astype(F32)
    ).astype(BF)
    grad_query, grad_key, grad_value, grad_out = finish(parts[OWN], a_got, parts[4 + OWN], b_got)
    return grad_in, grad_query, grad_key, grad_value, grad_out


def solution(mesh):
    fine = Mesh(mesh.devices.reshape(NX, NZ, NC, NT), ("x", "z", "c", "tp"))
    column = P(None, "tp")
    both = P(CTX, "tp")
    return jax.shard_map(
        on_device,
        mesh=fine,
        in_specs=(P(CTX, None), column, column, column, column, P(CTX, None), P(), P(), P()),
        out_specs=(both,) * 5,
        check_vma=False,
    )
```

profile of v0, /device:TPU:0, one launch (start us, length us, event | category | flops | bytes accessed | tf_op | source)
XLA Modules:
  0.0 181.7 jit_solution(13844380771432854251)
XLA Ops:
  0.6 12.6 %project.1 = (bf16[32,32,1280]{2,1,0:T(8,128)(2,1)}, f32[8,128]{1,0:T(8,128)}) custom-call(s32[1]{0:T(128)} %bitcast.me, s32[2048]{0:T(1024)} %piece_doc.1, s32[2048]{0:T(1024)} %piece_offset.1, s32[128]{0:T(128)} %doc_owner.1, bf16[512,4096]{1,0:T(8,128)(2,1)} %x_ref.1, bf16[512,4096]{1,0:T(8,128)(2,1)} %c_ref.1, bf16[4096,512]{1,0:T(8,128)(2,1)} %wq_ref.3, ...), custom_call_target="tpu_custom_call" | custom-call | flops 6000000000 | bytes 24000000 | tf_op jit(solution)/shard_map/project/pallas_call | solution.py:201
  13.3 8.5 %all-to-all-start = ((bf16[32,32,1280]{2,1,0:T(8,128)(2,1)}), bf16[32,32,1280]{2,1,0:T(8,128)(2,1)}, u32[]{:S(2)}, u32[]{:S(2)}) async-start(bf16[32,32,1280]{2,1,0:T(8,128)(2,1)} %get-tuple-element.50), calls=%async_computation | async-start | bytes 5242880 | tf_op jit(solution)/shard_map/all_to_all | solution.py:578
  21.8 2.2 %copy-done.3 = bf16[4096,512]{1,0:T(8,128)(2,1)S(1)} copy-done((bf16[4096,512]{1,0:T(8,128)(2,1)S(1)}, bf16[4096,512]{1,0:T(8,128)(2,1)}, u32[]{:S(2)}) %copy-start.3) | copy-done | bytes 4194328
  27.0 2.1 %copy-done.2 = bf16[3072,768]{1,0:T(8,128)(2,1)} copy-done((bf16[3072,768]{1,0:T(8,128)(2,1)}, bf16[3072,768]{1,0:T(8,128)(2,1)S(1)}, u32[]{:S(2)}) %copy-start.2) | copy-done | bytes 4718616
  29.2 3.4 %regroup.1 = (bf16[16,512,128]{2,1,0:T(8,128)(2,1)S(1)}, bf16[16,512,128]{2,1,0:T(8,128)(2,1)S(1)}, bf16[16,512,128]{2,1,0:T(8,128)(2,1)S(1)}, bf16[16,512,128]{2,1,0:T(8,128)(2,1)S(1)}, f32[8,128]{1,0:T(8,128)S(1)}) custom-call(s32[4]{0:T(128)S(1)} %pad_add_fusion.where, f32[8,128]{1,0:T(8,128)S(1)} %copy-done.11, bf16[512,4096]{1,0:T(8,128)(2,1)S(1)} %copy-done.4, ...), custom_call_target="tpu_custom_call" | custom-call | flops 1 | bytes 17000000 | tf_op jit(solution)/shard_map/regroup/pallas_call | solution.py:244
  38.4 17.9 %all-to-all-done.got_ref = bf16[32,32,1280]{2,1,0:T(8,128)(2,1)} async-done(((bf16[32,32,1280]{2,1,0:T(8,128)(2,1)}), bf16[32,32,1280]{2,1,0:T(8,128)(2,1)}, u32[]{:S(2)}, u32[]{:S(2)}) %all-to-all-start) | async-done | bytes 2621472 | tf_op jit(solution)/shard_map/all_to_all | solution.py:578
  56.3 7.6 %attend.1 = bf16[32,32,1280]{2,1,0:T(8,128)(2,1)S(1)} custom-call(s32[16]{0:T(128)S(1)} %select_reduce_fusion.3.live, s32[64]{0:T(128)S(1)} %get-tuple-element.98.offsets, bf16[32,32,1280]{2,1,0:T(8,128)(2,1)} %all-to-all-done.got_ref, f32[512,128]{1,0:T(8,128)S(1)} %copy-done.15, f32[512,128]{1,0:T(8,128)S(1)} %copy-done.14, ...), custom_call_target="tpu_custom_call" | custom-call | flops 4000000000 | bytes 6000000 | tf_op jit(solution)/shard_map/attend/pallas_call | solution.py:332
  65.5 5.0 %all-to-all-start.1 = ((bf16[32,32,1280]{2,1,0:T(8,128)(2,1)}), bf16[32,32,1280]{2,1,0:T(8,128)(2,1)}, u32[]{:S(2)}, u32[]{:S(2)}) async-start(bf16[32,32,1280]{2,1,0:T(8,128)(2,1)} %copy-done.8), calls=%async_computation.1 | async-start | bytes 5242880 | tf_op jit(solution)/shard_map/all_to_all | solution.py:635
  71.9 33.1 %all-to-all-done.1.got_ref = bf16[32,32,1280]{2,1,0:T(8,128)(2,1)} async-done(((bf16[32,32,1280]{2,1,0:T(8,128)(2,1)}), bf16[32,32,1280]{2,1,0:T(8,128)(2,1)}, u32[]{:S(2)}, u32[]{:S(2)}) %all-to-all-start.1) | async-done | bytes 2621472 | tf_op jit(solution)/shard_map/all_to_all | solution.py:635
  105.0 2.9 %restore.1.after.dy_ref.own = bf16[512,1280]{1,0:T(8,128)(2,1)S(1)} custom-call(s32[16]{0:T(128)S(1)} %select_reduce_fusion.4.targets, bf16[32,32,1280]{2,1,0:T(8,128)(2,1)} %all-to-all-done.1.got_ref, s32[1,512]{1,0:T(1,128)S(1)} %add.104.rows_ref), custom_call_target="tpu_custom_call" | custom-call | flops 700000000 | bytes 4000000 | tf_op jit(solution)/shard_map/restore/pallas_call | solution.py:391
  109.1 2.0 %collective-permute-done.peer = bf16[512,1280]{1,0:T(8,128)(2,1)S(1)} collective-permute-done((bf16[512,1280]{1,0:T(8,128)(2,1)S(1)}, bf16[512,1280]{1,0:T(8,128)(2,1)S(1)}, u32[]{:S(2)}, u32[]{:S(2)}) %collective-permute-start) | collective-permute-done | bytes 1310752 | tf_op jit(solution)/shard_map/ppermute | solution.py:560
  111.1 2.9 %weight_grad.3 = (bf16[320,512]{1,0:T(8,128)(2,1)S(1)}, bf16[320,512]{1,0:T(8,128)(2,1)S(1)}, bf16[320,512]{1,0:T(8,128)(2,1)S(1)}, bf16[320,512]{1,0:T(8,128)(2,1)S(1)}) custom-call(bf16[256,1024]{1,0:T(8,128)(2,1)S(1)} %get-tuple-element.75.after, bf16[512,1280]{1,0:T(8,128)(2,1)S(1)} %restore.1.after.dy_ref.own, ...), custom_call_target="tpu_custom_call" | custom-call | flops 1400000000 | bytes 6000000 | tf_op jit(solution)/shard_map/weight_grad/pallas_call | solution.py:472
  114.7 3.0 %collective-permute-start.6 = (bf16[320,512]{1,0:T(8,128)(2,1)S(1)}, bf16[320,512]{1,0:T(8,128)(2,1)S(1)}, u32[]{:S(2)}, u32[]{:S(2)}) collective-permute-start(bf16[320,512]{1,0:T(8,128)(2,1)S(1)} %get-tuple-element.71), channel_id=1, source_target_pairs={{0,24},{8,0},{16,8},{24,16},{1,25},{9,1},{17,9},{25,17},{2,26},{10... | collective-permute-start | bytes 983048 | tf_op jit(solution)/shard_map/ppermute | solution.py:560
  117.6 1.7 collective-permute-start.3
  119.4 4.6 %weight_grad.4 = (bf16[1280,512]{1,0:T(8,128)(2,1)S(1)}, bf16[1280,512]{1,0:T(8,128)(2,1)S(1)}) custom-call(bf16[320,512]{1,0:T(8,128)(2,1)S(1)} %get-tuple-element.66.after, bf16[512,1280]{1,0:T(8,128)(2,1)S(1)} %restore.1.after.dy_ref.own, bf16[512,1280]{1,0:T(8,128)(2,1)S(1)} %collective-permute-done.peer, ...), custom_call_target="tpu_custom_call" | custom-call | flops 2800000000 | bytes 12000000 | tf_op jit(solution)/shard_map/weight_grad/pallas_call | solution.py:472
  125.1 2.7 %collective-permute-done.3.refs_1_ = bf16[320,512]{1,0:T(8,128)(2,1)S(1)} collective-permute-done((bf16[320,512]{1,0:T(8,128)(2,1)S(1)}, bf16[320,512]{1,0:T(8,128)(2,1)S(1)}, u32[]{:S(2)}, u32[]{:S(2)}) %collective-permute-start.3) | collective-permute-done | bytes 327712 | tf_op jit(solution)/shard_map/ppermute | solution.py:560
  128.2 1.6 collective-permute-start.7
  129.9 1.7 collective-permute-start.8
  131.6 2.0 %input_grad.4.after.refs_0_ = bf16[1024,1024]{1,0:T(8,128)(2,1)S(1)} custom-call(bf16[640,512]{1,0:T(8,128)(2,1)S(1)} %get-tuple-element.72.after, bf16[512,1280]{1,0:T(8,128)(2,1)S(1)} %restore.1.after.dy_ref.own, bf16[3072,768]{1,0:T(8,128)(2,1)S(1)} %bitcast.7), custom_call_target="tpu_custom_call" | custom-call | flops 1600000000 | bytes 10000000 | tf_op jit(solution)/shard_map/input_grad/pallas_call | solution.py:420
  133.6 8.3 %collective-permute-done.7.refs_1_ = bf16[256,1024]{1,0:T(8,128)(2,1)S(1)} collective-permute-done((bf16[256,1024]{1,0:T(8,128)(2,1)S(1)}, bf16[256,1024]{1,0:T(8,128)(2,1)S(1)}, u32[]{:S(2)}, u32[]{:S(2)}) %collective-permute-start.7) | collective-permute-done | bytes 524320 | tf_op jit(solution)/shard_map/ppermute | solution.py:560
  142.2 1.6 collective-permute-start.9
  143.8 1.7 collective-permute-start.10
  145.5 3.2 %collective-permute-start.14 = (bf16[640,512]{1,0:T(8,128)(2,1)S(1)}, bf16[640,512]{1,0:T(8,128)(2,1)S(1)}, u32[]{:S(2)}, u32[]{:S(2)}) collective-permute-start(bf16[640,512]{1,0:T(8,128)(2,1)S(1)} %get-tuple-element.82), channel_id=1, source_target_pairs={{0,24},{8,0},{16,8},{24,16},{1,25},{9,1},{17,9},{25,17},{2,26},{10... | collective-permute-start | bytes 1966088 | tf_op jit(solution)/shard_map/ppermute | solution.py:560
  148.8 1.7 collective-permute-start.11
  150.4 2.9 %weight_grad.5 = (bf16[640,512]{1,0:T(8,128)(2,1)S(1)}, bf16[640,512]{1,0:T(8,128)(2,1)S(1)}) custom-call(bf16[1024,1024]{1,0:T(8,128)(2,1)S(1)} %input_grad.4.after.refs_0_, bf16[512,1280]{1,0:T(8,128)(2,1)S(1)} %restore.1.after.dy_ref.own, bf16[512,1280]{1,0:T(8,128)(2,1)S(1)} %collective-permute-done.peer, ...), custom_call_target="tpu_custom_call" | custom-call | flops 1400000000 | bytes 6000000 | tf_op jit(solution)/shard_map/weight_grad/pallas_call | solution.py:472
  153.3 7.1 %collective-permute-done.13.up_b = bf16[640,512]{1,0:T(8,128)(2,1)S(1)} collective-permute-done((bf16[640,512]{1,0:T(8,128)(2,1)S(1)}, bf16[640,512]{1,0:T(8,128)(2,1)S(1)}, u32[]{:S(2)}, u32[]{:S(2)}) %collective-permute-start.13) | collective-permute-done | bytes 655392 | tf_op jit(solution)/shard_map/ppermute | solution.py:560
  160.5 2.7 %collective-permute-done.11.up_a = bf16[640,512]{1,0:T(8,128)(2,1)S(1)} collective-permute-done((bf16[640,512]{1,0:T(8,128)(2,1)S(1)}, bf16[640,512]{1,0:T(8,128)(2,1)S(1)}, u32[]{:S(2)}, u32[]{:S(2)}) %collective-permute-start.11) | collective-permute-done | bytes 655392 | tf_op jit(solution)/shard_map/ppermute | solution.py:560
  164.9 2.2 %collective-permute-start.17 = (bf16[640,128]{1,0:T(8,128)(2,1)S(1)}, bf16[640,128]{1,0:T(8,128)(2,1)S(1)}, u32[]{:S(2)}, u32[]{:S(2)}) collective-permute-start(bf16[640,128]{1,0:T(8,128)(2,1)S(1)} %get-tuple-element.86), channel_id=1, source_target_pairs={{0,24},{8,0},{16,8},{24,16},{1,25},{9,1},{17,9},{25,17},{2,26},{10... | collective-permute-start | bytes 491528 | tf_op jit(solution)/shard_map/ppermute | solution.py:560
  167.0 3.6 %collective-permute-done.15.refs_1_ = bf16[640,128]{1,0:T(8,128)(2,1)S(1)} collective-permute-done((bf16[640,128]{1,0:T(8,128)(2,1)S(1)}, bf16[640,128]{1,0:T(8,128)(2,1)S(1)}, u32[]{:S(2)}, u32[]{:S(2)}) %collective-permute-start.15) | collective-permute-done | bytes 163872 | tf_op jit(solution)/shard_map/ppermute | solution.py:560
  172.3 3.1 %collective-permute-start.20 = (bf16[640,128]{1,0:T(8,128)(2,1)S(1)}, bf16[640,128]{1,0:T(8,128)(2,1)S(1)}, u32[]{:S(2)}, u32[]{:S(2)}) collective-permute-start(bf16[640,128]{1,0:T(8,128)(2,1)S(1)} %get-tuple-element.90), channel_id=1, source_target_pairs={{0,96},{32,0},{64,32},{96,64},{1,97},{33,1},{65,33},{97,65},{2,98}... | collective-permute-start | bytes 491528 | tf_op jit(solution)/shard_map/ppermute | solution.py:560
  177.5 1.7 collective-permute-done.19.refs_6_
  180.1 1.6 add_convert_fusion
  (101 shorter events, 21.8 us)
Async XLA Ops:
  13.2 8.6 %copy-start.6 = (bf16[4096,128]{1,0:T(8,128)(2,1)S(1)}, bf16[4096,128]{1,0:T(8,128)(2,1)}, u32[]{:S(2)}) copy-start(bf16[4096,128]{1,0:T(8,128)(2,1)} %wk_ref.3) | copy-start | bytes 3145732
  13.2 8.6 %copy-start.7 = (bf16[4096,128]{1,0:T(8,128)(2,1)S(1)}, bf16[4096,128]{1,0:T(8,128)(2,1)}, u32[]{:S(2)}) copy-start(bf16[4096,128]{1,0:T(8,128)(2,1)} %wv_ref.3) | copy-start | bytes 3145732
  13.3 8.6 %copy-start.11 = (f32[8,128]{1,0:T(8,128)S(1)}, f32[8,128]{1,0:T(8,128)}, u32[]{:S(2)}) copy-start(f32[8,128]{1,0:T(8,128)} %get-tuple-element.51.after) | copy-start | bytes 12292
  13.3 43.0 %all-to-all-start = ((bf16[32,32,1280]{2,1,0:T(8,128)(2,1)}), bf16[32,32,1280]{2,1,0:T(8,128)(2,1)}, u32[]{:S(2)}, u32[]{:S(2)}) async-start(bf16[32,32,1280]{2,1,0:T(8,128)(2,1)} %get-tuple-element.50), calls=%async_computation | async-start | bytes 5242880 | tf_op jit(solution)/shard_map/all_to_all | solution.py:578
  29.1 7.6 %copy-start.18 = (s32[128]{0:T(128)S(1)}, s32[128]{0:T(128)}, u32[]{:S(2)}) copy-start(s32[128]{0:T(128)} %doc_owner.1) | copy-start | bytes 1540
  29.1 8.3 %copy-start.17 = (s32[2048]{0:T(1024)S(1)}, s32[2048]{0:T(1024)}, u32[]{:S(2)}) copy-start(s32[2048]{0:T(1024)} %piece_offset.1) | copy-start | bytes 24580
  29.2 27.1 %copy-start.14 = (f32[512,128]{1,0:T(8,128)S(1)}, f32[512,128]{1,0:T(8,128)}, u32[]{:S(2)}) copy-start(f32[512,128]{1,0:T(8,128)} %constant.40.clone.sin_table) | copy-start | bytes 786436
  29.2 27.1 %copy-start.15 = (f32[512,128]{1,0:T(8,128)S(1)}, f32[512,128]{1,0:T(8,128)}, u32[]{:S(2)}) copy-start(f32[512,128]{1,0:T(8,128)} %constant.39.clone.cos_table) | copy-start | bytes 786436
  65.5 39.6 %all-to-all-start.1 = ((bf16[32,32,1280]{2,1,0:T(8,128)(2,1)}), bf16[32,32,1280]{2,1,0:T(8,128)(2,1)}, u32[]{:S(2)}, u32[]{:S(2)}) async-start(bf16[32,32,1280]{2,1,0:T(8,128)(2,1)} %copy-done.8), calls=%async_computation.1 | async-start | bytes 5242880 | tf_op jit(solution)/shard_map/all_to_all | solution.py:635
  70.5 38.7 %collective-permute-start.1 = (bf16[16,512,128]{2,1,0:T(8,128)(2,1)}, bf16[16,512,128]{2,1,0:T(8,128)(2,1)}, u32[]{:S(2)}, u32[]{:S(2)}) collective-permute-start(bf16[16,512,128]{2,1,0:T(8,128)(2,1)} %copy-done.13), channel_id=1, source_target_pairs={{0,4},{4,0},{1,5},{5,1},{2,6},{6,2},{3,7},{7,3},{8,12},{12,8},{9,1... | collective-permute-start | bytes 6291464 | tf_op jit(solution)/shard_map/ppermute | solution.py:560
  70.6 38.5 %collective-permute-start.2 = (bf16[16,512,128]{2,1,0:T(8,128)(2,1)}, bf16[16,512,128]{2,1,0:T(8,128)(2,1)}, u32[]{:S(2)}, u32[]{:S(2)}) collective-permute-start(bf16[16,512,128]{2,1,0:T(8,128)(2,1)} %copy-done.12), channel_id=1, source_target_pairs={{0,4},{4,0},{1,5},{5,1},{2,6},{6,2},{3,7},{7,3},{8,12},{12,8},{9,1... | collective-permute-start | bytes 6291464 | tf_op jit(solution)/shard_map/ppermute | solution.py:560
  108.0 3.1 %collective-permute-start = (bf16[512,1280]{1,0:T(8,128)(2,1)S(1)}, bf16[512,1280]{1,0:T(8,128)(2,1)S(1)}, u32[]{:S(2)}, u32[]{:S(2)}) collective-permute-start(bf16[512,1280]{1,0:T(8,128)(2,1)S(1)} %restore.1.after.dy_ref.own), channel_id=1, source_target_pairs={{0,4},{4,0},{1,5},{5,1},{2,6},{6,2},{3,7},{7,3},{8,12},{12,8},{9,1... | collective-permute-start | bytes 3932168 | tf_op jit(solution)/shard_map/ppermute | solution.py:560
  114.0 17.5 %slice-start = ((s8[4718592]{0:T(1024)(128)(4,1)}), s8[4194304]{0:T(1024)(128)(4,1)S(1)}, s32[]{:S(2)}) async-start(s8[4718592]{0:T(1024)(128)(4,1)} %bitcast.6), calls=%async_computation.2 | async-start | bytes 8388608
  114.0 17.5 %slice-start.1 = ((s8[4718592]{0:T(1024)(128)(4,1)}), s8[524288]{0:T(1024)(128)(4,1)S(1)}, s32[]{:S(2)}) async-start(s8[4718592]{0:T(1024)(128)(4,1)} %bitcast.6), calls=%async_computation.3 | async-start | bytes 1048576
  114.0 9.9 %collective-permute-start.4 = (bf16[320,512]{1,0:T(8,128)(2,1)S(1)}, bf16[320,512]{1,0:T(8,128)(2,1)S(1)}, u32[]{:S(2)}, u32[]{:S(2)}) collective-permute-start(bf16[320,512]{1,0:T(8,128)(2,1)S(1)} %get-tuple-element.68), channel_id=1, source_target_pairs={{0,96},{32,0},{64,32},{96,64},{1,97},{33,1},{65,33},{97,65},{2,98}... | collective-permute-start | bytes 983048 | tf_op jit(solution)/shard_map/ppermute | solution.py:560
  114.4 10.7 %collective-permute-start.5 = (bf16[320,512]{1,0:T(8,128)(2,1)S(1)}, bf16[320,512]{1,0:T(8,128)(2,1)S(1)}, u32[]{:S(2)}, u32[]{:S(2)}) collective-permute-start(bf16[320,512]{1,0:T(8,128)(2,1)S(1)} %get-tuple-element.70), channel_id=1, source_target_pairs={{0,8},{8,16},{16,24},{24,0},{1,9},{9,17},{17,25},{25,1},{2,10},{10... | collective-permute-start | bytes 983048 | tf_op jit(solution)/shard_map/ppermute | solution.py:560
  114.7 10.5 %collective-permute-start.6 = (bf16[320,512]{1,0:T(8,128)(2,1)S(1)}, bf16[320,512]{1,0:T(8,128)(2,1)S(1)}, u32[]{:S(2)}, u32[]{:S(2)}) collective-permute-start(bf16[320,512]{1,0:T(8,128)(2,1)S(1)} %get-tuple-element.71), channel_id=1, source_target_pairs={{0,24},{8,0},{16,8},{24,16},{1,25},{9,1},{17,9},{25,17},{2,26},{10... | collective-permute-start | bytes 983048 | tf_op jit(solution)/shard_map/ppermute | solution.py:560
  117.6 10.2 %collective-permute-start.3 = (bf16[320,512]{1,0:T(8,128)(2,1)S(1)}, bf16[320,512]{1,0:T(8,128)(2,1)S(1)}, u32[]{:S(2)}, u32[]{:S(2)}) collective-permute-start(bf16[320,512]{1,0:T(8,128)(2,1)S(1)} %get-tuple-element.66.after), channel_id=1, source_target_pairs={{0,32},{32,64},{64,96},{96,0},{1,33},{33,65},{65,97},{97,1},{2,34}... | collective-permute-start | bytes 983048 | tf_op jit(solution)/shard_map/ppermute | solution.py:560
  128.2 20.6 %collective-permute-start.12 = (bf16[640,512]{1,0:T(8,128)(2,1)S(1)}, bf16[640,512]{1,0:T(8,128)(2,1)S(1)}, u32[]{:S(2)}, u32[]{:S(2)}) collective-permute-start(bf16[640,512]{1,0:T(8,128)(2,1)S(1)} %get-tuple-element.79), channel_id=1, source_target_pairs={{0,96},{32,0},{64,32},{96,64},{1,97},{33,1},{65,33},{97,65},{2,98}... | collective-permute-start | bytes 1966088 | tf_op jit(solution)/shard_map/ppermute | solution.py:560
  128.2 13.7 %collective-permute-start.7 = (bf16[256,1024]{1,0:T(8,128)(2,1)S(1)}, bf16[256,1024]{1,0:T(8,128)(2,1)S(1)}, u32[]{:S(2)}, u32[]{:S(2)}) collective-permute-start(bf16[256,1024]{1,0:T(8,128)(2,1)S(1)} %get-tuple-element.75.after), channel_id=1, source_target_pairs={{0,1},{1,2},{2,3},{3,0},{4,5},{5,6},{6,7},{7,4},{8,9},{9,10},{10,1... | collective-permute-start | bytes 1572872 | tf_op jit(solution)/shard_map/ppermute | solution.py:560
  129.9 12.0 %collective-permute-start.8 = (bf16[256,1024]{1,0:T(8,128)(2,1)S(1)}, bf16[256,1024]{1,0:T(8,128)(2,1)S(1)}, u32[]{:S(2)}, u32[]{:S(2)}) collective-permute-start(bf16[256,1024]{1,0:T(8,128)(2,1)S(1)} %get-tuple-element.76), channel_id=1, source_target_pairs={{0,3},{1,0},{2,1},{3,2},{4,7},{5,4},{6,5},{7,6},{8,11},{9,8},{10,9... | collective-permute-start | bytes 1572872 | tf_op jit(solution)/shard_map/ppermute | solution.py:560
  142.2 37.9 %collective-permute-start.9 = (bf16[512,1024]{1,0:T(8,128)(2,1)S(1)}, bf16[512,1024]{1,0:T(8,128)(2,1)S(1)}, u32[]{:S(2)}, u32[]{:S(2)}) collective-permute-start(bf16[512,1024]{1,0:T(8,128)(2,1)S(1)} %get-tuple-element.77), channel_id=1, source_target_pairs={{0,1},{1,2},{2,3},{3,0},{4,5},{5,6},{6,7},{7,4},{8,9},{9,10},{10,1... | collective-permute-start | bytes 3145736 | tf_op jit(solution)/shard_map/ppermute | solution.py:560
  143.8 36.3 %collective-permute-start.10 = (bf16[512,1024]{1,0:T(8,128)(2,1)S(1)}, bf16[512,1024]{1,0:T(8,128)(2,1)S(1)}, u32[]{:S(2)}, u32[]{:S(2)}) collective-permute-start(bf16[512,1024]{1,0:T(8,128)(2,1)S(1)} %get-tuple-element.78), channel_id=1, source_target_pairs={{0,3},{1,0},{2,1},{3,2},{4,7},{5,4},{6,5},{7,6},{8,11},{9,8},{10,9... | collective-permute-start | bytes 3145736 | tf_op jit(solution)/shard_map/ppermute | solution.py:560
  145.5 15.0 %collective-permute-start.13 = (bf16[640,512]{1,0:T(8,128)(2,1)S(1)}, bf16[640,512]{1,0:T(8,128)(2,1)S(1)}, u32[]{:S(2)}, u32[]{:S(2)}) collective-permute-start(bf16[640,512]{1,0:T(8,128)(2,1)S(1)} %get-tuple-element.81), channel_id=1, source_target_pairs={{0,8},{8,16},{16,24},{24,0},{1,9},{9,17},{17,25},{25,1},{2,10},{10... | collective-permute-start | bytes 1966088 | tf_op jit(solution)/shard_map/ppermute | solution.py:560
  145.5 15.0 %collective-permute-start.14 = (bf16[640,512]{1,0:T(8,128)(2,1)S(1)}, bf16[640,512]{1,0:T(8,128)(2,1)S(1)}, u32[]{:S(2)}, u32[]{:S(2)}) collective-permute-start(bf16[640,512]{1,0:T(8,128)(2,1)S(1)} %get-tuple-element.82), channel_id=1, source_target_pairs={{0,24},{8,0},{16,8},{24,16},{1,25},{9,1},{17,9},{25,17},{2,26},{10... | collective-permute-start | bytes 1966088 | tf_op jit(solution)/shard_map/ppermute | solution.py:560
  148.8 14.4 %collective-permute-start.11 = (bf16[640,512]{1,0:T(8,128)(2,1)S(1)}, bf16[640,512]{1,0:T(8,128)(2,1)S(1)}, u32[]{:S(2)}, u32[]{:S(2)}) collective-permute-start(bf16[640,512]{1,0:T(8,128)(2,1)S(1)} %get-tuple-element.72.after), channel_id=1, source_target_pairs={{0,32},{32,64},{64,96},{96,0},{1,33},{33,65},{65,97},{97,1},{2,34}... | collective-permute-start | bytes 1966088 | tf_op jit(solution)/shard_map/ppermute | solution.py:560
  163.6 7.0 %collective-permute-start.15 = (bf16[640,128]{1,0:T(8,128)(2,1)S(1)}, bf16[640,128]{1,0:T(8,128)(2,1)S(1)}, u32[]{:S(2)}, u32[]{:S(2)}) collective-permute-start(bf16[640,128]{1,0:T(8,128)(2,1)S(1)} %get-tuple-element.84), channel_id=1, source_target_pairs={{0,16},{8,24},{16,0},{24,8},{1,17},{9,25},{17,1},{25,9},{2,18},{10... | collective-permute-start | bytes 491528 | tf_op jit(solution)/shard_map/ppermute | solution.py:560
  163.7 8.4 %collective-permute-start.16 = (bf16[640,128]{1,0:T(8,128)(2,1)S(1)}, bf16[640,128]{1,0:T(8,128)(2,1)S(1)}, u32[]{:S(2)}, u32[]{:S(2)}) collective-permute-start(bf16[640,128]{1,0:T(8,128)(2,1)S(1)} %get-tuple-element.85), channel_id=1, source_target_pairs={{0,8},{8,16},{16,24},{24,0},{1,9},{9,17},{17,25},{25,1},{2,10},{10... | collective-permute-start | bytes 491528 | tf_op jit(solution)/shard_map/ppermute | solution.py:560
  164.9 7.4 %collective-permute-start.17 = (bf16[640,128]{1,0:T(8,128)(2,1)S(1)}, bf16[640,128]{1,0:T(8,128)(2,1)S(1)}, u32[]{:S(2)}, u32[]{:S(2)}) collective-permute-start(bf16[640,128]{1,0:T(8,128)(2,1)S(1)} %get-tuple-element.86), channel_id=1, source_target_pairs={{0,24},{8,0},{16,8},{24,16},{1,25},{9,1},{17,9},{25,17},{2,26},{10... | collective-permute-start | bytes 491528 | tf_op jit(solution)/shard_map/ppermute | solution.py:560
  170.6 6.9 %collective-permute-start.18 = (bf16[640,128]{1,0:T(8,128)(2,1)S(1)}, bf16[640,128]{1,0:T(8,128)(2,1)S(1)}, u32[]{:S(2)}, u32[]{:S(2)}) collective-permute-start(bf16[640,128]{1,0:T(8,128)(2,1)S(1)} %get-tuple-element.88), channel_id=1, source_target_pairs={{0,64},{32,96},{64,0},{96,32},{1,65},{33,97},{65,1},{97,33},{2,66}... | collective-permute-start | bytes 491528 | tf_op jit(solution)/shard_map/ppermute | solution.py:560
  172.1 7.1 %collective-permute-start.19 = (bf16[640,128]{1,0:T(8,128)(2,1)S(1)}, bf16[640,128]{1,0:T(8,128)(2,1)S(1)}, u32[]{:S(2)}, u32[]{:S(2)}) collective-permute-start(bf16[640,128]{1,0:T(8,128)(2,1)S(1)} %get-tuple-element.89), channel_id=1, source_target_pairs={{0,32},{32,64},{64,96},{96,0},{1,33},{33,65},{65,97},{97,1},{2,34}... | collective-permute-start | bytes 491528 | tf_op jit(solution)/shard_map/ppermute | solution.py:560
  172.3 7.0 %collective-permute-start.20 = (bf16[640,128]{1,0:T(8,128)(2,1)S(1)}, bf16[640,128]{1,0:T(8,128)(2,1)S(1)}, u32[]{:S(2)}, u32[]{:S(2)}) collective-permute-start(bf16[640,128]{1,0:T(8,128)(2,1)S(1)} %get-tuple-element.90), channel_id=1, source_target_pairs={{0,96},{32,0},{64,32},{96,64},{1,97},{33,1},{65,33},{97,65},{2,98}... | collective-permute-start | bytes 491528 | tf_op jit(solution)/shard_map/ppermute | solution.py:560
  (12 other events, 33.0 us)
where the time goes:
time: 182 us
  waiting for transfers between devices  82.4 us (45%)
  Pallas kernels  44.7 us (25%)
  starting transfers between devices  38.2 us (21%)
  local copies, waits for them, and re-layouts  11.9 us (7%)
  other arithmetic  3.29 us (2%)
    all_to_all x1, waiting for transfers between devices, on_device(): home = lax.all_to_all(back, CTX, split_axis=0, concat_axis=0, tiled=True)  33.1 us
    ppermute x21, waiting for transfers between devices, shift(): return lax.ppermute(value, axis, [(i, (i + by) % n) for i in range(n)])  31.4 us
    ppermute x21, starting transfers between devices, shift(): return lax.ppermute(value, axis, [(i, (i + by) % n) for i in range(n)])  24.8 us
    all_to_all x1, waiting for transfers between devices, on_device(): got = lax.all_to_all(sent, CTX, split_axis=0, concat_axis=0, tiled=True)  17.9 us
    pallas_call x1, Pallas kernels, project(): pl.pallas_call(project_kernel, in_specs=[smem_spec()] * 4 + [any_spec()]...  12.6 us
    unnamed x42, local copies, waits for them, and re-layouts  11.1 us
    pallas_call x3, Pallas kernels, weight_grad(): pl.pallas_call(weight_grad_kernel, grid=(count,), in_specs=[any_spec(), p...  10.3 us
    all_to_all x1, starting transfers between devices, on_device(): got = lax.all_to_all(sent, CTX, split_axis=0, concat_axis=0, tiled=True)  8.45 us
  transfers between devices with their start and end apart: 23, of which 12 were waited for; matrix products, arithmetic and copies ran while one was open for 1% of the time, Pallas kernels for 12%

commit v1 on v0

--- a/solution.py
+++ b/solution.py
@@ -380,11 +380,15 @@
 
 def restore_kernel(targets, got_ref, rows_ref, out_ref, packed, sems):
     copies = fetch_blocks(got_ref, targets, packed, sems)
-    slot = lax.broadcasted_iota(I32, (TOK, TOK), 0)
+    slot = lax.broadcasted_iota(I32, (TOK, TOK), 1)
     one_hot = jnp.where(slot == rows_ref[...], 1.0, 0.0).astype(BF)
-    for copy in copies:
+    cut = TOK // 2
+    for copy in copies[: TARGETS // 2]:
         copy.wait()
-    out_ref[...] = dot(one_hot, packed[...], TN).astype(BF)
+    total = dot(one_hot[:, :cut], packed[:cut, :])
+    for copy in copies[TARGETS // 2 :]:
+        copy.wait()
+    out_ref[...] = (total + dot(one_hot[:, cut:], packed[cut:, :])).astype(BF)
 
 
 def restore(targets, got, rows):
@@ -534,7 +538,8 @@
 
 
 def finish_kernel(*refs):
-    ins, (query, key, value, out) = refs[:8], refs[8:]
+    ins, (rows, query, key, value, out) = refs[:11], refs[11:]
+    rows[...] = sum(ref[...].astype(F32) for ref in ins[8:]).astype(BF)
     a, b = (sum(ref[...].astype(F32) for ref in ins[4 * g : 4 * g + 4]).T for g in range(2))
     value[...] = a[:, :KW].astype(BF)
     out[...] = a[:, KW:].astype(BF)
@@ -542,17 +547,17 @@
     key[...] = b[:, QW:].astype(BF)
 
 
-def finish(own_a, got_a, own_b, got_b):
+def finish(own_a, got_a, own_b, got_b, own_y, got_y):
     shape = lambda n: jax.ShapeDtypeStruct((HEAD, n), BF)
     return pl.pallas_call(
         finish_kernel,
-        in_specs=[vmem_spec()] * 8,
-        out_specs=[vmem_spec()] * 4,
-        out_shape=[shape(QW), shape(KW), shape(KW), shape(QW)],
+        in_specs=[vmem_spec()] * 11,
+        out_specs=[vmem_spec()] * 5,
+        out_shape=[jax.ShapeDtypeStruct(own_y.shape, BF), shape(QW), shape(KW), shape(KW), shape(QW)],
         compiler_params=params(16),
-        cost_estimate=cost(1e6, 2e6),
+        cost_estimate=cost(1e6, 6e6),
         name="finish",
-    )(own_a, *got_a, own_b, *got_b)
+    )(own_a, *got_a, own_b, *got_b, own_y, *got_y)
 
 
 def shift(value, axis, by):
@@ -564,8 +569,11 @@
     return shift(up, axis, 1), shift(down, axis, -1)
 
 
-def all_ways(parts, axis):
-    return shift(parts[FAR], axis, 2), shift(parts[UP], axis, 1), shift(parts[DOWN], axis, -1)
+def all_ways(a, a_axis, b, b_axis):
+    far = shift(a[FAR], a_axis, 2), shift(b[FAR], b_axis, 2)
+    up = shift(a[UP], a_axis, 1), shift(b[UP], b_axis, 1)
+    down = shift(a[DOWN], a_axis, -1), shift(b[DOWN], b_axis, -1)
+    return tuple(zip(far, up, down))
 
 
 def on_device(x, wq, wk, wv, wo, c, piece_doc, piece_offset, doc_owner):
@@ -593,7 +601,7 @@
     blocks = jnp.arange(TARGETS, dtype=I32) * (PAIR // PIECE)
     targets = jnp.sum(jnp.where(blocks[:, None] == slot[None, :], own_owner[None, :], 0), axis=1)
     within = jnp.arange(PIECE, dtype=I32)
-    packed_row = (slot[:, None] * PIECE + within[None, :]).reshape(1, TOK)
+    packed_row = (slot[:, None] * PIECE + within[None, :]).reshape(TOK, 1)
 
     mine_doc = doc_owner == me
     doc_rank = jnp.sum((mine_doc[None, :] & (doc_ids[None, :] < doc_ids[:, None])).astype(I32), axis=1)
@@ -636,27 +644,24 @@
     dy = restore(targets, home, packed_row)
     peer = shift(dy, "c", 1)
     y0, y1 = input_grad(dy, 0, 1, dy, w_far, split=True)
+    y_far = both_ways(y0, y1, "tp")
     a0, a1, b0, b1 = weight_grad(y0, FAR, 1, True, dy, peer, xk, xr, ck, cr)
-    y0, y1, a0, a1, b0, b1 = lax.optimization_barrier((y0, y1, a0, a1, b0, b1))
     a_far = both_ways(a0, a1, "x")
     b_far = both_ways(b0, b1, "z")
-    y_far = both_ways(y0, y1, "tp")
     a_near, b_near = weight_grad(a0, UP, 2, False, dy, peer, xk, xr, ck, cr)
+    y_near = input_grad(a_near, UP - 1, 2, dy, w_rest)
     sums = add_near((a_near, *a_far), (b_near, *b_far))
     a_got = both_ways(*sums[:2], "x")
     b_got = both_ways(*sums[2:], "z")
-    y_near = input_grad(sums[0], UP - 1, 2, dy, w_rest)
     y_sums = add_near((y_near, *y_far))
     y_got = both_ways(*y_sums, "tp")
     a_own, b_own = weight_grad(y_near, OWN, 1, False, dy, peer, xk, xr, ck, cr)
     y_own = input_grad(a_own, OWN - 1, 1, dy, w_rest)
     parts = add_total(a_own, a_got, b_own, b_got)
-    a_got = all_ways(parts[:4], "z")
-    b_got = all_ways(parts[4:], "x")
-    grad_in = (
-        y_own.astype(F32) + y_got[0].astype(F32) + y_got[1].astype(F32)
-    ).astype(BF)
-    grad_query, grad_key, grad_value, grad_out = finish(parts[OWN], a_got, parts[4 + OWN], b_got)
+    a_got, b_got = all_ways(parts[:4], "z", parts[4:], "x")
+    grad_in, grad_query, grad_key, grad_value, grad_out = finish(
+        parts[OWN], a_got, parts[4 + OWN], b_got, y_own, y_got
+    )
     return grad_in, grad_query, grad_key, grad_value, grad_out
 
 

time: 182 us -> 179 us (0.984)
  waiting for transfers between devices: 82.4 us -> 80.2 us
    ppermute x21, waiting for transfers between devices: 31.4 us -> 29.2 us  [shift(): return lax.ppermute(value, axis, [(i, (i + by) % n) for i in range(n)])]
where the time goes in v1:
time: 179 us
  waiting for transfers between devices  80.2 us (45%)
  Pallas kernels  45.7 us (26%)
  starting transfers between devices  37.9 us (21%)
  local copies, waits for them, and re-layouts  12 us (7%)
    all_to_all x1, waiting for transfers between devices, on_device(): home = lax.all_to_all(back, CTX, split_axis=0, concat_axis=0, tiled=True)  33.1 us
    ppermute x21, waiting for transfers between devices, shift(): return lax.ppermute(value, axis, [(i, (i + by) % n) for i in range(n)])  29.2 us
    ppermute x21, starting transfers between devices, shift(): return lax.ppermute(value, axis, [(i, (i + by) % n) for i in range(n)])  24.4 us
    all_to_all x1, waiting for transfers between devices, on_device(): got = lax.all_to_all(sent, CTX, split_axis=0, concat_axis=0, tiled=True)  17.9 us
    pallas_call x1, Pallas kernels, project(): pl.pallas_call(project_kernel, in_specs=[smem_spec()] * 4 + [any_spec()]...  12.6 us
    unnamed x42, local copies, waits for them, and re-layouts  11.1 us
    pallas_call x3, Pallas kernels, weight_grad(): pl.pallas_call(weight_grad_kernel, grid=(count,), in_specs=[any_spec(), p...  10.3 us
    all_to_all x1, starting transfers between devices, on_device(): got = lax.all_to_all(sent, CTX, split_axis=0, concat_axis=0, tiled=True)  8.47 us
  transfers between devices with their start and end apart: 23, of which 12 were waited for; matrix products, arithmetic and copies ran while one was open for 1% of the time, Pallas kernels for 12%

profile of v1, /device:TPU:0, one launch (start us, length us, event | category | flops | bytes accessed | tf_op | source)
XLA Modules:
  0.0 178.6 jit_solution(15472671738981071922)
XLA Ops:
  0.6 12.6 %project.1 = (bf16[32,32,1280]{2,1,0:T(8,128)(2,1)}, f32[8,128]{1,0:T(8,128)}) custom-call(s32[1]{0:T(128)} %bitcast.me, s32[2048]{0:T(1024)} %piece_doc.1, s32[2048]{0:T(1024)} %piece_offset.1, s32[128]{0:T(128)} %doc_owner.1, bf16[512,4096]{1,0:T(8,128)(2,1)} %x_ref.1, bf16[512,4096]{1,0:T(8,128)(2,1)} %c_ref.1, bf16[4096,512]{1,0:T(8,128)(2,1)} %wq_ref.3, ...), custom_call_target="tpu_custom_call" | custom-call | flops 6000000000 | bytes 24000000 | tf_op jit(solution)/shard_map/project/pallas_call | solution.py:201
  13.2 8.5 %all-to-all-start = ((bf16[32,32,1280]{2,1,0:T(8,128)(2,1)}), bf16[32,32,1280]{2,1,0:T(8,128)(2,1)}, u32[]{:S(2)}, u32[]{:S(2)}) async-start(bf16[32,32,1280]{2,1,0:T(8,128)(2,1)} %get-tuple-element.40), calls=%async_computation | async-start | bytes 5242880 | tf_op jit(solution)/shard_map/all_to_all | solution.py:586
  21.8 2.2 %copy-done.3 = bf16[4096,512]{1,0:T(8,128)(2,1)S(1)} copy-done((bf16[4096,512]{1,0:T(8,128)(2,1)S(1)}, bf16[4096,512]{1,0:T(8,128)(2,1)}, u32[]{:S(2)}) %copy-start.3) | copy-done | bytes 4194328
  27.0 2.1 %copy-done.2 = bf16[3072,768]{1,0:T(8,128)(2,1)} copy-done((bf16[3072,768]{1,0:T(8,128)(2,1)}, bf16[3072,768]{1,0:T(8,128)(2,1)S(1)}, u32[]{:S(2)}) %copy-start.2) | copy-done | bytes 4718616
  29.2 3.4 %regroup.1 = (bf16[16,512,128]{2,1,0:T(8,128)(2,1)S(1)}, bf16[16,512,128]{2,1,0:T(8,128)(2,1)S(1)}, bf16[16,512,128]{2,1,0:T(8,128)(2,1)S(1)}, bf16[16,512,128]{2,1,0:T(8,128)(2,1)S(1)}, f32[8,128]{1,0:T(8,128)S(1)}) custom-call(s32[4]{0:T(128)S(1)} %pad_add_fusion.where, f32[8,128]{1,0:T(8,128)S(1)} %copy-done.11, bf16[512,4096]{1,0:T(8,128)(2,1)S(1)} %copy-done.4, ...), custom_call_target="tpu_custom_call" | custom-call | flops 1 | bytes 17000000 | tf_op jit(solution)/shard_map/regroup/pallas_call | solution.py:244
  38.4 17.9 %all-to-all-done.got_ref = bf16[32,32,1280]{2,1,0:T(8,128)(2,1)} async-done(((bf16[32,32,1280]{2,1,0:T(8,128)(2,1)}), bf16[32,32,1280]{2,1,0:T(8,128)(2,1)}, u32[]{:S(2)}, u32[]{:S(2)}) %all-to-all-start) | async-done | bytes 2621472 | tf_op jit(solution)/shard_map/all_to_all | solution.py:586
  56.3 7.6 %attend.1 = bf16[32,32,1280]{2,1,0:T(8,128)(2,1)S(1)} custom-call(s32[16]{0:T(128)S(1)} %select_reduce_fusion.3.live, s32[64]{0:T(128)S(1)} %get-tuple-element.78.offsets, bf16[32,32,1280]{2,1,0:T(8,128)(2,1)} %all-to-all-done.got_ref, f32[512,128]{1,0:T(8,128)S(1)} %copy-done.15, f32[512,128]{1,0:T(8,128)S(1)} %copy-done.14, ...), custom_call_target="tpu_custom_call" | custom-call | flops 4000000000 | bytes 6000000 | tf_op jit(solution)/shard_map/attend/pallas_call | solution.py:332
  63.9 1.6 copy-done.8
  65.5 5.0 %all-to-all-start.1 = ((bf16[32,32,1280]{2,1,0:T(8,128)(2,1)}), bf16[32,32,1280]{2,1,0:T(8,128)(2,1)}, u32[]{:S(2)}, u32[]{:S(2)}) async-start(bf16[32,32,1280]{2,1,0:T(8,128)(2,1)} %copy-done.8), calls=%async_computation.1 | async-start | bytes 5242880 | tf_op jit(solution)/shard_map/all_to_all | solution.py:643
  71.9 33.1 %all-to-all-done.1.got_ref = bf16[32,32,1280]{2,1,0:T(8,128)(2,1)} async-done(((bf16[32,32,1280]{2,1,0:T(8,128)(2,1)}), bf16[32,32,1280]{2,1,0:T(8,128)(2,1)}, u32[]{:S(2)}, u32[]{:S(2)}) %all-to-all-start.1) | async-done | bytes 2621472 | tf_op jit(solution)/shard_map/all_to_all | solution.py:643
  105.0 2.9 %restore.1.after.dy_ref.own = bf16[512,1280]{1,0:T(8,128)(2,1)S(1)} custom-call(s32[16]{0:T(128)S(1)} %select_reduce_fusion.4.targets, bf16[32,32,1280]{2,1,0:T(8,128)(2,1)} %all-to-all-done.1.got_ref, s32[512,1]{1,0:T(8,128)S(1)} %add.100.rows_ref), custom_call_target="tpu_custom_call" | custom-call | flops 700000000 | bytes 4000000 | tf_op jit(solution)/shard_map/restore/pallas_call | solution.py:395
  109.1 2.0 %collective-permute-done.peer = bf16[512,1280]{1,0:T(8,128)(2,1)S(1)} collective-permute-done((bf16[512,1280]{1,0:T(8,128)(2,1)S(1)}, bf16[512,1280]{1,0:T(8,128)(2,1)S(1)}, u32[]{:S(2)}, u32[]{:S(2)}) %collective-permute-start) | collective-permute-done | bytes 1310752 | tf_op jit(solution)/shard_map/ppermute | solution.py:565
  111.1 2.9 %weight_grad.3 = (bf16[320,512]{1,0:T(8,128)(2,1)S(1)}, bf16[320,512]{1,0:T(8,128)(2,1)S(1)}, bf16[320,512]{1,0:T(8,128)(2,1)S(1)}, bf16[320,512]{1,0:T(8,128)(2,1)S(1)}) custom-call(bf16[256,1024]{1,0:T(8,128)(2,1)S(1)} %get-tuple-element.46.after, bf16[512,1280]{1,0:T(8,128)(2,1)S(1)} %restore.1.after.dy_ref.own, ...), custom_call_target="tpu_custom_call" | custom-call | flops 1400000000 | bytes 6000000 | tf_op jit(solution)/shard_map/weight_grad/pallas_call | solution.py:476
  114.6 3.0 %collective-permute-start.6 = (bf16[320,512]{1,0:T(8,128)(2,1)S(1)}, bf16[320,512]{1,0:T(8,128)(2,1)S(1)}, u32[]{:S(2)}, u32[]{:S(2)}) collective-permute-start(bf16[320,512]{1,0:T(8,128)(2,1)S(1)} %get-tuple-element.58), channel_id=1, source_target_pairs={{0,24},{8,0},{16,8},{24,16},{1,25},{9,1},{17,9},{25,17},{2,26},{10... | collective-permute-start | bytes 983048 | tf_op jit(solution)/shard_map/ppermute | solution.py:565
  117.6 1.7 collective-permute-start.3
  119.3 1.6 collective-permute-start.17
  120.9 2.9 %collective-permute-done.4.refs_2_ = bf16[320,512]{1,0:T(8,128)(2,1)S(1)} collective-permute-done((bf16[320,512]{1,0:T(8,128)(2,1)S(1)}, bf16[320,512]{1,0:T(8,128)(2,1)S(1)}, u32[]{:S(2)}, u32[]{:S(2)}) %collective-permute-start.4) | collective-permute-done | bytes 327712 | tf_op jit(solution)/shard_map/ppermute | solution.py:565
  123.8 3.0 %collective-permute-start.18 = (bf16[256,1024]{1,0:T(8,128)(2,1)S(1)}, bf16[256,1024]{1,0:T(8,128)(2,1)S(1)}, u32[]{:S(2)}, u32[]{:S(2)}) collective-permute-start(bf16[256,1024]{1,0:T(8,128)(2,1)S(1)} %get-tuple-element.72), channel_id=1, source_target_pairs={{0,3},{1,0},{2,1},{3,2},{4,7},{5,4},{6,5},{7,6},{8,11},{9,8},{10,9... | collective-permute-start | bytes 1572872 | tf_op jit(solution)/shard_map/ppermute | solution.py:565
  126.8 4.6 %weight_grad.4 = (bf16[1280,512]{1,0:T(8,128)(2,1)S(1)}, bf16[1280,512]{1,0:T(8,128)(2,1)S(1)}) custom-call(bf16[320,512]{1,0:T(8,128)(2,1)S(1)} %get-tuple-element.51.after, bf16[512,1280]{1,0:T(8,128)(2,1)S(1)} %restore.1.after.dy_ref.own, bf16[512,1280]{1,0:T(8,128)(2,1)S(1)} %collective-permute-done.peer, ...), custom_call_target="tpu_custom_call" | custom-call | flops 2800000000 | bytes 12000000 | tf_op jit(solution)/shard_map/weight_grad/pallas_call | solution.py:476
  131.9 2.1 %input_grad.4.after.refs_0_ = bf16[1024,1024]{1,0:T(8,128)(2,1)S(1)} custom-call(bf16[1280,512]{1,0:T(8,128)(2,1)S(1)} %get-tuple-element.52.after.refs_0_, bf16[512,1280]{1,0:T(8,128)(2,1)S(1)} %restore.1.after.dy_ref.own, bf16[3072,768]{1,0:T(8,128)(2,1)S(1)} %bitcast.7), custom_call_target="tpu_custom_call" | custom-call | flops 1600000000 | bytes 10000000 | tf_op jit(solution)/shard_map/input_grad/pallas_call | solution.py:424
  133.9 3.5 %collective-permute-done.18.refs_2_ = bf16[256,1024]{1,0:T(8,128)(2,1)S(1)} collective-permute-done((bf16[256,1024]{1,0:T(8,128)(2,1)S(1)}, bf16[256,1024]{1,0:T(8,128)(2,1)S(1)}, u32[]{:S(2)}, u32[]{:S(2)}) %collective-permute-start.18) | collective-permute-done | bytes 524320 | tf_op jit(solution)/shard_map/ppermute | solution.py:565
  138.8 2.7 %collective-permute-start.20 = (bf16[512,1024]{1,0:T(8,128)(2,1)S(1)}, bf16[512,1024]{1,0:T(8,128)(2,1)S(1)}, u32[]{:S(2)}, u32[]{:S(2)}) collective-permute-start(bf16[512,1024]{1,0:T(8,128)(2,1)S(1)} %get-tuple-element.74), channel_id=1, source_target_pairs={{0,3},{1,0},{2,1},{3,2},{4,7},{5,4},{6,5},{7,6},{8,11},{9,8},{10,9... | collective-permute-start | bytes 3145736 | tf_op jit(solution)/shard_map/ppermute | solution.py:565
  143.4 5.2 %collective-permute-done.7.up_a = bf16[640,512]{1,0:T(8,128)(2,1)S(1)} collective-permute-done((bf16[640,512]{1,0:T(8,128)(2,1)S(1)}, bf16[640,512]{1,0:T(8,128)(2,1)S(1)}, u32[]{:S(2)}, u32[]{:S(2)}) %collective-permute-start.7) | collective-permute-done | bytes 655392 | tf_op jit(solution)/shard_map/ppermute | solution.py:565
  149.7 2.9 %weight_grad.5 = (bf16[640,512]{1,0:T(8,128)(2,1)S(1)}, bf16[640,512]{1,0:T(8,128)(2,1)S(1)}) custom-call(bf16[1024,1024]{1,0:T(8,128)(2,1)S(1)} %input_grad.4.after.refs_0_, bf16[512,1280]{1,0:T(8,128)(2,1)S(1)} %restore.1.after.dy_ref.own, bf16[512,1280]{1,0:T(8,128)(2,1)S(1)} %collective-permute-done.peer, ...), custom_call_target="tpu_custom_call" | custom-call | flops 1400000000 | bytes 6000000 | tf_op jit(solution)/shard_map/weight_grad/pallas_call | solution.py:476
  152.6 3.7 %collective-permute-done.8.down_a = bf16[640,512]{1,0:T(8,128)(2,1)S(1)} collective-permute-done((bf16[640,512]{1,0:T(8,128)(2,1)S(1)}, bf16[640,512]{1,0:T(8,128)(2,1)S(1)}, u32[]{:S(2)}, u32[]{:S(2)}) %collective-permute-start.8) | collective-permute-done | bytes 655392 | tf_op jit(solution)/shard_map/ppermute | solution.py:565
  156.3 2.5 %collective-permute-done.9.up_b = bf16[640,512]{1,0:T(8,128)(2,1)S(1)} collective-permute-done((bf16[640,512]{1,0:T(8,128)(2,1)S(1)}, bf16[640,512]{1,0:T(8,128)(2,1)S(1)}, u32[]{:S(2)}, u32[]{:S(2)}) %collective-permute-start.9) | collective-permute-done | bytes 655392 | tf_op jit(solution)/shard_map/ppermute | solution.py:565
  158.8 4.7 %collective-permute-done.10.down_b = bf16[640,512]{1,0:T(8,128)(2,1)S(1)} collective-permute-done((bf16[640,512]{1,0:T(8,128)(2,1)S(1)}, bf16[640,512]{1,0:T(8,128)(2,1)S(1)}, u32[]{:S(2)}, u32[]{:S(2)}) %collective-permute-start.10) | collective-permute-done | bytes 655392 | tf_op jit(solution)/shard_map/ppermute | solution.py:565
  164.9 2.3 %collective-permute-start.12 = (bf16[640,128]{1,0:T(8,128)(2,1)S(1)}, bf16[640,128]{1,0:T(8,128)(2,1)S(1)}, u32[]{:S(2)}, u32[]{:S(2)}) collective-permute-start(bf16[640,128]{1,0:T(8,128)(2,1)S(1)} %get-tuple-element.66), channel_id=1, source_target_pairs={{0,8},{8,16},{16,24},{24,0},{1,9},{9,17},{17,25},{25,1},{2,10},{10... | collective-permute-start | bytes 491528 | tf_op jit(solution)/shard_map/ppermute | solution.py:565
  168.4 1.8 %collective-permute-start.15 = (bf16[640,128]{1,0:T(8,128)(2,1)S(1)}, bf16[640,128]{1,0:T(8,128)(2,1)S(1)}, u32[]{:S(2)}, u32[]{:S(2)}) collective-permute-start(bf16[640,128]{1,0:T(8,128)(2,1)S(1)} %get-tuple-element.70), channel_id=1, source_target_pairs={{0,32},{32,64},{64,96},{96,0},{1,33},{33,65},{65,97},{97,1},{2,34}... | collective-permute-start | bytes 491528 | tf_op jit(solution)/shard_map/ppermute | solution.py:565
  172.7 2.4 %collective-permute-done.14.refs_5_ = bf16[640,128]{1,0:T(8,128)(2,1)S(1)} collective-permute-done((bf16[640,128]{1,0:T(8,128)(2,1)S(1)}, bf16[640,128]{1,0:T(8,128)(2,1)S(1)}, u32[]{:S(2)}, u32[]{:S(2)}) %collective-permute-start.14) | collective-permute-done | bytes 163872 | tf_op jit(solution)/shard_map/ppermute | solution.py:565
  175.1 1.6 collective-permute-done.15.refs_6_
  176.7 1.9 %finish.1 = (bf16[512,1024]{1,0:T(8,128)(2,1)}, bf16[128,512]{1,0:T(8,128)(2,1)}, bf16[128,128]{1,0:T(8,128)(2,1)}, bf16[128,128]{1,0:T(8,128)(2,1)}, bf16[128,512]{1,0:T(8,128)(2,1)}) custom-call(f32[640,128]{1,0:T(8,128)S(1)} %get-tuple-element.64.refs_0_, bf16[640,128]{1,0:T(8,128)(2,1)S(1)} %collective-permute-done.11.refs_1_, ...), custom_call_target="tpu_custom_call" | custom-call | flops 1000000 | bytes 6000000 | tf_op jit(solution)/shard_map/finish/pallas_call | solution.py:552
  (100 shorter events, 21.8 us)
Async XLA Ops:
  13.2 8.6 %copy-start.6 = (bf16[4096,128]{1,0:T(8,128)(2,1)S(1)}, bf16[4096,128]{1,0:T(8,128)(2,1)}, u32[]{:S(2)}) copy-start(bf16[4096,128]{1,0:T(8,128)(2,1)} %wk_ref.3) | copy-start | bytes 3145732
  13.2 8.6 %copy-start.7 = (bf16[4096,128]{1,0:T(8,128)(2,1)S(1)}, bf16[4096,128]{1,0:T(8,128)(2,1)}, u32[]{:S(2)}) copy-start(bf16[4096,128]{1,0:T(8,128)(2,1)} %wv_ref.3) | copy-start | bytes 3145732
  13.2 8.6 %copy-start.11 = (f32[8,128]{1,0:T(8,128)S(1)}, f32[8,128]{1,0:T(8,128)}, u32[]{:S(2)}) copy-start(f32[8,128]{1,0:T(8,128)} %get-tuple-element.41.after) | copy-start | bytes 12292
  13.2 43.0 %all-to-all-start = ((bf16[32,32,1280]{2,1,0:T(8,128)(2,1)}), bf16[32,32,1280]{2,1,0:T(8,128)(2,1)}, u32[]{:S(2)}, u32[]{:S(2)}) async-start(bf16[32,32,1280]{2,1,0:T(8,128)(2,1)} %get-tuple-element.40), calls=%async_computation | async-start | bytes 5242880 | tf_op jit(solution)/shard_map/all_to_all | solution.py:586
  29.1 7.5 %copy-start.18 = (s32[128]{0:T(128)S(1)}, s32[128]{0:T(128)}, u32[]{:S(2)}) copy-start(s32[128]{0:T(128)} %doc_owner.1) | copy-start | bytes 1540
  29.2 8.3 %copy-start.17 = (s32[2048]{0:T(1024)S(1)}, s32[2048]{0:T(1024)}, u32[]{:S(2)}) copy-start(s32[2048]{0:T(1024)} %piece_offset.1) | copy-start | bytes 24580
  29.2 27.1 %copy-start.14 = (f32[512,128]{1,0:T(8,128)S(1)}, f32[512,128]{1,0:T(8,128)}, u32[]{:S(2)}) copy-start(f32[512,128]{1,0:T(8,128)} %constant.40.clone.sin_table) | copy-start | bytes 786436
  29.2 27.1 %copy-start.15 = (f32[512,128]{1,0:T(8,128)S(1)}, f32[512,128]{1,0:T(8,128)}, u32[]{:S(2)}) copy-start(f32[512,128]{1,0:T(8,128)} %constant.39.clone.cos_table) | copy-start | bytes 786436
  65.5 39.6 %all-to-all-start.1 = ((bf16[32,32,1280]{2,1,0:T(8,128)(2,1)}), bf16[32,32,1280]{2,1,0:T(8,128)(2,1)}, u32[]{:S(2)}, u32[]{:S(2)}) async-start(bf16[32,32,1280]{2,1,0:T(8,128)(2,1)} %copy-done.8), calls=%async_computation.1 | async-start | bytes 5242880 | tf_op jit(solution)/shard_map/all_to_all | solution.py:643
  70.5 38.6 %collective-permute-start.1 = (bf16[16,512,128]{2,1,0:T(8,128)(2,1)}, bf16[16,512,128]{2,1,0:T(8,128)(2,1)}, u32[]{:S(2)}, u32[]{:S(2)}) collective-permute-start(bf16[16,512,128]{2,1,0:T(8,128)(2,1)} %copy-done.13), channel_id=1, source_target_pairs={{0,4},{4,0},{1,5},{5,1},{2,6},{6,2},{3,7},{7,3},{8,12},{12,8},{9,1... | collective-permute-start | bytes 6291464 | tf_op jit(solution)/shard_map/ppermute | solution.py:565
  70.6 38.4 %collective-permute-start.2 = (bf16[16,512,128]{2,1,0:T(8,128)(2,1)}, bf16[16,512,128]{2,1,0:T(8,128)(2,1)}, u32[]{:S(2)}, u32[]{:S(2)}) collective-permute-start(bf16[16,512,128]{2,1,0:T(8,128)(2,1)} %copy-done.12), channel_id=1, source_target_pairs={{0,4},{4,0},{1,5},{5,1},{2,6},{6,2},{3,7},{7,3},{8,12},{12,8},{9,1... | collective-permute-start | bytes 6291464 | tf_op jit(solution)/shard_map/ppermute | solution.py:565
  107.9 3.1 %collective-permute-start = (bf16[512,1280]{1,0:T(8,128)(2,1)S(1)}, bf16[512,1280]{1,0:T(8,128)(2,1)S(1)}, u32[]{:S(2)}, u32[]{:S(2)}) collective-permute-start(bf16[512,1280]{1,0:T(8,128)(2,1)S(1)} %restore.1.after.dy_ref.own), channel_id=1, source_target_pairs={{0,4},{4,0},{1,5},{5,1},{2,6},{6,2},{3,7},{7,3},{8,12},{12,8},{9,1... | collective-permute-start | bytes 3932168 | tf_op jit(solution)/shard_map/ppermute | solution.py:565
  114.0 9.8 %collective-permute-start.4 = (bf16[320,512]{1,0:T(8,128)(2,1)S(1)}, bf16[320,512]{1,0:T(8,128)(2,1)S(1)}, u32[]{:S(2)}, u32[]{:S(2)}) collective-permute-start(bf16[320,512]{1,0:T(8,128)(2,1)S(1)} %get-tuple-element.55), channel_id=1, source_target_pairs={{0,96},{32,0},{64,32},{96,64},{1,97},{33,1},{65,33},{97,65},{2,98}... | collective-permute-start | bytes 983048 | tf_op jit(solution)/shard_map/ppermute | solution.py:565
  114.3 17.0 %collective-permute-start.5 = (bf16[320,512]{1,0:T(8,128)(2,1)S(1)}, bf16[320,512]{1,0:T(8,128)(2,1)S(1)}, u32[]{:S(2)}, u32[]{:S(2)}) collective-permute-start(bf16[320,512]{1,0:T(8,128)(2,1)S(1)} %get-tuple-element.57), channel_id=1, source_target_pairs={{0,8},{8,16},{16,24},{24,0},{1,9},{9,17},{17,25},{25,1},{2,10},{10... | collective-permute-start | bytes 983048 | tf_op jit(solution)/shard_map/ppermute | solution.py:565
  114.6 16.8 %collective-permute-start.6 = (bf16[320,512]{1,0:T(8,128)(2,1)S(1)}, bf16[320,512]{1,0:T(8,128)(2,1)S(1)}, u32[]{:S(2)}, u32[]{:S(2)}) collective-permute-start(bf16[320,512]{1,0:T(8,128)(2,1)S(1)} %get-tuple-element.58), channel_id=1, source_target_pairs={{0,24},{8,0},{16,8},{24,16},{1,25},{9,1},{17,9},{25,17},{2,26},{10... | collective-permute-start | bytes 983048 | tf_op jit(solution)/shard_map/ppermute | solution.py:565
  117.6 13.8 %collective-permute-start.3 = (bf16[320,512]{1,0:T(8,128)(2,1)S(1)}, bf16[320,512]{1,0:T(8,128)(2,1)S(1)}, u32[]{:S(2)}, u32[]{:S(2)}) collective-permute-start(bf16[320,512]{1,0:T(8,128)(2,1)S(1)} %get-tuple-element.51.after), channel_id=1, source_target_pairs={{0,32},{32,64},{64,96},{96,0},{1,33},{33,65},{65,97},{97,1},{2,34}... | collective-permute-start | bytes 983048 | tf_op jit(solution)/shard_map/ppermute | solution.py:565
  119.3 18.1 %collective-permute-start.17 = (bf16[256,1024]{1,0:T(8,128)(2,1)S(1)}, bf16[256,1024]{1,0:T(8,128)(2,1)S(1)}, u32[]{:S(2)}, u32[]{:S(2)}) collective-permute-start(bf16[256,1024]{1,0:T(8,128)(2,1)S(1)} %get-tuple-element.46.after), channel_id=1, source_target_pairs={{0,1},{1,2},{2,3},{3,0},{4,5},{5,6},{6,7},{7,4},{8,9},{9,10},{10,1... | collective-permute-start | bytes 1572872 | tf_op jit(solution)/shard_map/ppermute | solution.py:565
  123.8 8.1 %slice-start = ((s8[4718592]{0:T(1024)(128)(4,1)}), s8[4194304]{0:T(1024)(128)(4,1)S(1)}, s32[]{:S(2)}) async-start(s8[4718592]{0:T(1024)(128)(4,1)} %bitcast.6), calls=%async_computation.2 | async-start | bytes 8388608
  123.8 8.1 %slice-start.1 = ((s8[4718592]{0:T(1024)(128)(4,1)}), s8[524288]{0:T(1024)(128)(4,1)S(1)}, s32[]{:S(2)}) async-start(s8[4718592]{0:T(1024)(128)(4,1)} %bitcast.6), calls=%async_computation.3 | async-start | bytes 1048576
  123.8 13.6 %collective-permute-start.18 = (bf16[256,1024]{1,0:T(8,128)(2,1)S(1)}, bf16[256,1024]{1,0:T(8,128)(2,1)S(1)}, u32[]{:S(2)}, u32[]{:S(2)}) collective-permute-start(bf16[256,1024]{1,0:T(8,128)(2,1)S(1)} %get-tuple-element.72), channel_id=1, source_target_pairs={{0,3},{1,0},{2,1},{3,2},{4,7},{5,4},{6,5},{7,6},{8,11},{9,8},{10,9... | collective-permute-start | bytes 1572872 | tf_op jit(solution)/shard_map/ppermute | solution.py:565
  131.7 16.9 %collective-permute-start.7 = (bf16[640,512]{1,0:T(8,128)(2,1)S(1)}, bf16[640,512]{1,0:T(8,128)(2,1)S(1)}, u32[]{:S(2)}, u32[]{:S(2)}) collective-permute-start(bf16[640,512]{1,0:T(8,128)(2,1)S(1)} %get-tuple-element.59), channel_id=1, source_target_pairs={{0,32},{32,64},{64,96},{96,0},{1,33},{33,65},{65,97},{97,1},{2,34}... | collective-permute-start | bytes 1966088 | tf_op jit(solution)/shard_map/ppermute | solution.py:565
  137.7 30.5 %collective-permute-start.19 = (bf16[512,1024]{1,0:T(8,128)(2,1)S(1)}, bf16[512,1024]{1,0:T(8,128)(2,1)S(1)}, u32[]{:S(2)}, u32[]{:S(2)}) collective-permute-start(bf16[512,1024]{1,0:T(8,128)(2,1)S(1)} %get-tuple-element.73), channel_id=1, source_target_pairs={{0,1},{1,2},{2,3},{3,0},{4,5},{5,6},{6,7},{7,4},{8,9},{9,10},{10,1... | collective-permute-start | bytes 3145736 | tf_op jit(solution)/shard_map/ppermute | solution.py:565
  138.8 29.6 %collective-permute-start.20 = (bf16[512,1024]{1,0:T(8,128)(2,1)S(1)}, bf16[512,1024]{1,0:T(8,128)(2,1)S(1)}, u32[]{:S(2)}, u32[]{:S(2)}) collective-permute-start(bf16[512,1024]{1,0:T(8,128)(2,1)S(1)} %get-tuple-element.74), channel_id=1, source_target_pairs={{0,3},{1,0},{2,1},{3,2},{4,7},{5,4},{6,5},{7,6},{8,11},{9,8},{10,9... | collective-permute-start | bytes 3145736 | tf_op jit(solution)/shard_map/ppermute | solution.py:565
  141.5 14.8 %collective-permute-start.8 = (bf16[640,512]{1,0:T(8,128)(2,1)S(1)}, bf16[640,512]{1,0:T(8,128)(2,1)S(1)}, u32[]{:S(2)}, u32[]{:S(2)}) collective-permute-start(bf16[640,512]{1,0:T(8,128)(2,1)S(1)} %get-tuple-element.60), channel_id=1, source_target_pairs={{0,96},{32,0},{64,32},{96,64},{1,97},{33,1},{65,33},{97,65},{2,98}... | collective-permute-start | bytes 1966088 | tf_op jit(solution)/shard_map/ppermute | solution.py:565
  143.1 15.7 %collective-permute-start.9 = (bf16[640,512]{1,0:T(8,128)(2,1)S(1)}, bf16[640,512]{1,0:T(8,128)(2,1)S(1)}, u32[]{:S(2)}, u32[]{:S(2)}) collective-permute-start(bf16[640,512]{1,0:T(8,128)(2,1)S(1)} %get-tuple-element.62), channel_id=1, source_target_pairs={{0,8},{8,16},{16,24},{24,0},{1,9},{9,17},{17,25},{25,1},{2,10},{10... | collective-permute-start | bytes 1966088 | tf_op jit(solution)/shard_map/ppermute | solution.py:565
  148.7 14.8 %collective-permute-start.10 = (bf16[640,512]{1,0:T(8,128)(2,1)S(1)}, bf16[640,512]{1,0:T(8,128)(2,1)S(1)}, u32[]{:S(2)}, u32[]{:S(2)}) collective-permute-start(bf16[640,512]{1,0:T(8,128)(2,1)S(1)} %get-tuple-element.63), channel_id=1, source_target_pairs={{0,24},{8,0},{16,8},{24,16},{1,25},{9,1},{17,9},{25,17},{2,26},{10... | collective-permute-start | bytes 1966088 | tf_op jit(solution)/shard_map/ppermute | solution.py:565
  163.9 7.0 %collective-permute-start.11 = (bf16[640,128]{1,0:T(8,128)(2,1)S(1)}, bf16[640,128]{1,0:T(8,128)(2,1)S(1)}, u32[]{:S(2)}, u32[]{:S(2)}) collective-permute-start(bf16[640,128]{1,0:T(8,128)(2,1)S(1)} %get-tuple-element.65), channel_id=1, source_target_pairs={{0,16},{8,24},{16,0},{24,8},{1,17},{9,25},{17,1},{25,9},{2,18},{10... | collective-permute-start | bytes 491528 | tf_op jit(solution)/shard_map/ppermute | solution.py:565
  164.9 7.7 %collective-permute-start.12 = (bf16[640,128]{1,0:T(8,128)(2,1)S(1)}, bf16[640,128]{1,0:T(8,128)(2,1)S(1)}, u32[]{:S(2)}, u32[]{:S(2)}) collective-permute-start(bf16[640,128]{1,0:T(8,128)(2,1)S(1)} %get-tuple-element.66), channel_id=1, source_target_pairs={{0,8},{8,16},{16,24},{24,0},{1,9},{9,17},{17,25},{25,1},{2,10},{10... | collective-permute-start | bytes 491528 | tf_op jit(solution)/shard_map/ppermute | solution.py:565
  167.3 5.4 %collective-permute-start.13 = (bf16[640,128]{1,0:T(8,128)(2,1)S(1)}, bf16[640,128]{1,0:T(8,128)(2,1)S(1)}, u32[]{:S(2)}, u32[]{:S(2)}) collective-permute-start(bf16[640,128]{1,0:T(8,128)(2,1)S(1)} %get-tuple-element.67), channel_id=1, source_target_pairs={{0,24},{8,0},{16,8},{24,16},{1,25},{9,1},{17,9},{25,17},{2,26},{10... | collective-permute-start | bytes 491528 | tf_op jit(solution)/shard_map/ppermute | solution.py:565
  168.2 6.9 %collective-permute-start.14 = (bf16[640,128]{1,0:T(8,128)(2,1)S(1)}, bf16[640,128]{1,0:T(8,128)(2,1)S(1)}, u32[]{:S(2)}, u32[]{:S(2)}) collective-permute-start(bf16[640,128]{1,0:T(8,128)(2,1)S(1)} %get-tuple-element.69), channel_id=1, source_target_pairs={{0,64},{32,96},{64,0},{96,32},{1,65},{33,97},{65,1},{97,33},{2,66}... | collective-permute-start | bytes 491528 | tf_op jit(solution)/shard_map/ppermute | solution.py:565
  168.4 8.3 %collective-permute-start.15 = (bf16[640,128]{1,0:T(8,128)(2,1)S(1)}, bf16[640,128]{1,0:T(8,128)(2,1)S(1)}, u32[]{:S(2)}, u32[]{:S(2)}) collective-permute-start(bf16[640,128]{1,0:T(8,128)(2,1)S(1)} %get-tuple-element.70), channel_id=1, source_target_pairs={{0,32},{32,64},{64,96},{96,0},{1,33},{33,65},{65,97},{97,1},{2,34}... | collective-permute-start | bytes 491528 | tf_op jit(solution)/shard_map/ppermute | solution.py:565
  170.9 5.8 %collective-permute-start.16 = (bf16[640,128]{1,0:T(8,128)(2,1)S(1)}, bf16[640,128]{1,0:T(8,128)(2,1)S(1)}, u32[]{:S(2)}, u32[]{:S(2)}) collective-permute-start(bf16[640,128]{1,0:T(8,128)(2,1)S(1)} %get-tuple-element.71), channel_id=1, source_target_pairs={{0,96},{32,0},{64,32},{96,64},{1,97},{33,1},{65,33},{97,65},{2,98}... | collective-permute-start | bytes 491528 | tf_op jit(solution)/shard_map/ppermute | solution.py:565
  (12 other events, 32.9 us)

commit v2 on v1

--- a/solution.py
+++ b/solution.py
@@ -378,7 +378,35 @@
     )(where, after, wq, wk, wv)
 
 
-def restore_kernel(targets, got_ref, rows_ref, out_ref, packed, sems):
+def collect_kernel(xk_hbm, xr_hbm, ck_hbm, cr_hbm, far_ref, token, sems):
+    token[...] = jnp.zeros_like(token)
+    pairs = []
+    for i, source in enumerate((xk_hbm, xr_hbm, ck_hbm, cr_hbm)):
+        pairs.append((source.at[pl.ds(FAR * NZ, NZ)], far_ref.at[pl.ds(i * NZ, NZ)]))
+    for i, source in enumerate((xk_hbm, xr_hbm)):
+        for j in range(NX):
+            pairs.append((source.at[j * NZ + FAR], far_ref.at[4 * NZ + i * NX + j]))
+    copies = [pltpu.make_async_copy(*pair, sems.at[n]) for n, pair in enumerate(pairs)]
+    for copy in copies:
+        copy.start()
+    for copy in copies:
+        copy.wait()
+
+
+def collect(xk, xr, ck, cr):
+    return pl.pallas_call(
+        collect_kernel,
+        in_specs=[any_spec()] * 4,
+        out_specs=[vmem_spec(), vmem_spec()],
+        out_shape=[jax.ShapeDtypeStruct((4 * NZ + 2 * NX, TOK, HEAD), BF), TOKEN],
+        scratch_shapes=[pltpu.SemaphoreType.DMA((4 + 2 * NX,))],
+        compiler_params=params(8),
+        cost_estimate=cost(1, 6e6),
+        name="collect",
+    )(xk, xr, ck, cr)
+
+
+def restore_kernel(targets, got_ref, rows_ref, token, out_ref, packed, sems):
     copies = fetch_blocks(got_ref, targets, packed, sems)
     slot = lax.broadcasted_iota(I32, (TOK, TOK), 1)
     one_hot = jnp.where(slot == rows_ref[...], 1.0, 0.0).astype(BF)
@@ -391,17 +419,42 @@
     out_ref[...] = (total + dot(one_hot[:, cut:], packed[cut:, :])).astype(BF)
 
 
-def restore(targets, got, rows):
+def restore(targets, got, rows, token):
     return pl.pallas_call(
         restore_kernel,
-        in_specs=[smem_spec(), any_spec(), vmem_spec()],
+        in_specs=[smem_spec(), any_spec(), vmem_spec(), any_spec()],
         out_specs=vmem_spec(),
         out_shape=jax.ShapeDtypeStruct((TOK, COLS), BF),
         scratch_shapes=[pltpu.VMEM((TOK, COLS), BF), pltpu.SemaphoreType.DMA((TARGETS,))],
         compiler_params=params(16),
         cost_estimate=cost(0.7e9, 4e6),
         name="restore",
-    )(targets, got, rows)
+    )(targets, got, rows, token)
+
+
+def weight_far_kernel(after, own, peer, far, a0, a1, b0, b1):
+    wide = lambda i: jnp.concatenate([far[4 * i + j] for j in range(NZ)], axis=1)
+    first = dot(own[:, V0:G0], wide(0), TN) + dot(peer[:, V0:G0], wide(1), TN)
+    a0[:KW, :] = first.astype(BF)
+    second = dot(own[:, G0:], wide(2), TN) + dot(peer[:, G0:], wide(3), TN)
+    a0[KW:, :] = second[: CUT - KW].astype(BF)
+    a1[...] = second[CUT - KW :].astype(BF)
+    third = dot(own[:, :V0], wide(4), TN) + dot(peer[:, :V0], wide(5), TN)
+    b0[...] = third[:CUT].astype(BF)
+    b1[...] = third[CUT:].astype(BF)
+
+
+def weight_far(after, own, peer, far):
+    shape = jax.ShapeDtypeStruct((CUT, NZ * HEAD), BF)
+    return pl.pallas_call(
+        weight_far_kernel,
+        in_specs=[any_spec()] + [vmem_spec()] * 3,
+        out_specs=[vmem_spec()] * 4,
+        out_shape=[shape] * 4,
+        compiler_params=params(20),
+        cost_estimate=cost(1.4e9, 6e6),
+        name="weight_far",
+    )(after, own, peer, far)
 
 
 def input_grad_kernel(after, dy_ref, w_ref, *outs):
@@ -445,21 +498,13 @@
     third = dot(own[:, :V0], join([b00, b01, b02, b03]), TN) + dot(
         peer[:, :V0], join([b10, b11, b12, b13]), TN
     )
-    if len(outs) == 4:
-        a0, a1, b0, b1 = outs
-        a0[:KW, :] = first.astype(BF)
-        a0[KW:, :] = second[: CUT - KW].astype(BF)
-        a1[...] = second[CUT - KW :].astype(BF)
-        b0[...] = third[:CUT].astype(BF)
-        b1[...] = third[CUT:].astype(BF)
-    else:
-        a, b = outs
-        a[:KW, :] = first.astype(BF)
-        a[KW:, :] = second.astype(BF)
-        b[...] = third.astype(BF)
-
-
-def weight_grad(after, at, count, split, own, peer, xk, xr, ck, cr):
+    a, b = outs
+    a[:KW, :] = first.astype(BF)
+    a[KW:, :] = second.astype(BF)
+    b[...] = third.astype(BF)
+
+
+def weight_grad(after, at, count, own, peer, xk, xr, ck, cr):
     wide = NZ * HEAD
     whole = lambda i: (0, 0)
     spec_a = pl.BlockSpec((NZ, TOK, HEAD), lambda i: (at + 2 * i, 0, 0))
@@ -467,12 +512,8 @@
         pl.BlockSpec((1, TOK, HEAD), functools.partial(lambda j, i: (j * NZ + at + 2 * i, 0, 0), j))
         for j in range(NX)
     ]
-    if split:
-        out_shape = [jax.ShapeDtypeStruct((CUT, wide), BF)] * 4
-        out_specs = [pl.BlockSpec((CUT, wide), whole)] * 4
-    else:
-        out_shape = [jax.ShapeDtypeStruct((count * HALF, wide), BF)] * 2
-        out_specs = [pl.BlockSpec((HALF, wide), lambda i: (i, 0))] * 2
+    out_shape = [jax.ShapeDtypeStruct((count * HALF, wide), BF)] * 2
+    out_specs = [pl.BlockSpec((HALF, wide), lambda i: (i, 0))] * 2
     return pl.pallas_call(
         weight_grad_kernel,
         grid=(count,),
@@ -641,21 +682,22 @@
         token_r,
     )
     home = lax.all_to_all(back, CTX, split_axis=0, concat_axis=0, tiled=True)
-    dy = restore(targets, home, packed_row)
+    far, token_c = collect(xk, xr, ck, cr)
+    dy = restore(targets, home, packed_row, token_c)
     peer = shift(dy, "c", 1)
     y0, y1 = input_grad(dy, 0, 1, dy, w_far, split=True)
     y_far = both_ways(y0, y1, "tp")
-    a0, a1, b0, b1 = weight_grad(y0, FAR, 1, True, dy, peer, xk, xr, ck, cr)
+    a0, a1, b0, b1 = weight_far(y0, dy, peer, far)
     a_far = both_ways(a0, a1, "x")
     b_far = both_ways(b0, b1, "z")
-    a_near, b_near = weight_grad(a0, UP, 2, False, dy, peer, xk, xr, ck, cr)
+    a_near, b_near = weight_grad(a0, UP, 2, dy, peer, xk, xr, ck, cr)
     y_near = input_grad(a_near, UP - 1, 2, dy, w_rest)
     sums = add_near((a_near, *a_far), (b_near, *b_far))
     a_got = both_ways(*sums[:2], "x")
     b_got = both_ways(*sums[2:], "z")
     y_sums = add_near((y_near, *y_far))
     y_got = both_ways(*y_sums, "tp")
-    a_own, b_own = weight_grad(y_near, OWN, 1, False, dy, peer, xk, xr, ck, cr)
+    a_own, b_own = weight_grad(y_near, OWN, 1, dy, peer, xk, xr, ck, cr)
     y_own = input_grad(a_own, OWN - 1, 1, dy, w_rest)
     parts = add_total(a_own, a_got, b_own, b_got)
     a_got, b_got = all_ways(parts[:4], "z", parts[4:], "x")

time: 179 us -> 178 us (level)
  waiting for transfers between devices: 80.2 us -> 75 us
  local copies, waits for them, and re-layouts: 12 us -> 15.2 us
    all_to_all x1, waiting for transfers between devices: 33.1 us -> 21.8 us  [on_device(): home = lax.all_to_all(back, CTX, split_axis=0, concat_axis=0, tiled=True)]
    ppermute x21, waiting for transfers between devices: 29.2 us -> 35.4 us  [shift(): return lax.ppermute(value, axis, [(i, (i + by) % n) for i in range(n)])]
    pallas_call x0 -> x2, Pallas kernels: none -> 3.51 us  [the longest x1 1.95 us: collect(): pl.pallas_call(collect_kernel, in_specs=[any_spec()] * 4, out_specs=[vmem...]
    unnamed x42 -> x48, local copies, waits for them, and re-layouts: 11.1 us -> 14.4 us
    pallas_call x3 -> x2, Pallas kernels: 10.3 us -> 7.45 us  [weight_grad(): pl.pallas_call(weight_grad_kernel, grid=(count,), in_specs=[any_spec(), p...]
  transfers between devices with their start and end apart: 23 -> 23, of which waited for: 12 -> 14; matrix products, arithmetic and copies ran while one was open for 1% -> 1% of each run, Pallas kernels for 12% -> 11%
where the time goes in v2:
time: 178 us; the launch traced here: 177 us
  waiting for transfers between devices  75 us (42%)
  Pallas kernels  46.3 us (26%)
  starting transfers between devices  37.8 us (21%)
  local copies, waits for them, and re-layouts  15.2 us (9%)
    ppermute x21, waiting for transfers between devices, shift(): return lax.ppermute(value, axis, [(i, (i + by) % n) for i in range(n)])  35.4 us
    ppermute x21, starting transfers between devices, shift(): return lax.ppermute(value, axis, [(i, (i + by) % n) for i in range(n)])  24.3 us
    all_to_all x1, waiting for transfers between devices, on_device(): home = lax.all_to_all(back, CTX, split_axis=0, concat_axis=0, tiled=True)  21.8 us
    all_to_all x1, waiting for transfers between devices, on_device(): got = lax.all_to_all(sent, CTX, split_axis=0, concat_axis=0, tiled=True)  17.8 us
    unnamed x48, local copies, waits for them, and re-layouts  14.4 us
    pallas_call x1, Pallas kernels, project(): pl.pallas_call(project_kernel, in_specs=[smem_spec()] * 4 + [any_spec()]...  12.6 us
    all_to_all x1, starting transfers between devices, on_device(): got = lax.all_to_all(sent, CTX, split_axis=0, concat_axis=0, tiled=True)  8.47 us
    pallas_call x1, Pallas kernels, attend(): pl.pallas_call(attend_kernel, in_specs=[smem_spec(), smem_spec(), any_spe...  7.6 us
  transfers between devices with their start and end apart: 23, of which 14 were waited for; matrix products, arithmetic and copies ran while one was open for 1% of the time, Pallas kernels for 11%

profile of v2, /device:TPU:0, one launch (start us, length us, event | category | flops | bytes accessed | tf_op | source)
XLA Modules:
  0.0 177.2 jit_solution(14120964950569156873)
XLA Ops:
  0.6 12.6 %project.1 = (bf16[32,32,1280]{2,1,0:T(8,128)(2,1)}, f32[8,128]{1,0:T(8,128)}) custom-call(s32[1]{0:T(128)} %bitcast.me, s32[2048]{0:T(1024)} %piece_doc.1, s32[2048]{0:T(1024)} %piece_offset.1, s32[128]{0:T(128)} %doc_owner.1, bf16[512,4096]{1,0:T(8,128)(2,1)} %x_ref.1, bf16[512,4096]{1,0:T(8,128)(2,1)} %c_ref.1, bf16[4096,512]{1,0:T(8,128)(2,1)} %wq_ref.3, ...), custom_call_target="tpu_custom_call" | custom-call | flops 6000000000 | bytes 24000000 | tf_op jit(solution)/shard_map/project/pallas_call | solution.py:201
  13.3 8.5 %all-to-all-start = ((bf16[32,32,1280]{2,1,0:T(8,128)(2,1)}), bf16[32,32,1280]{2,1,0:T(8,128)(2,1)}, u32[]{:S(2)}, u32[]{:S(2)}) async-start(bf16[32,32,1280]{2,1,0:T(8,128)(2,1)} %get-tuple-element.42), calls=%async_computation | async-start | bytes 5242880 | tf_op jit(solution)/shard_map/all_to_all | solution.py:627
  21.8 2.2 %copy-done.4 = bf16[4096,512]{1,0:T(8,128)(2,1)S(1)} copy-done((bf16[4096,512]{1,0:T(8,128)(2,1)S(1)}, bf16[4096,512]{1,0:T(8,128)(2,1)}, u32[]{:S(2)}) %copy-start.4) | copy-done | bytes 4194328
  27.1 2.1 %copy-done.3 = bf16[3072,768]{1,0:T(8,128)(2,1)} copy-done((bf16[3072,768]{1,0:T(8,128)(2,1)}, bf16[3072,768]{1,0:T(8,128)(2,1)S(1)}, u32[]{:S(2)}) %copy-start.3) | copy-done | bytes 4718616
  29.2 3.4 %regroup.1 = (bf16[16,512,128]{2,1,0:T(8,128)(2,1)S(1)}, bf16[16,512,128]{2,1,0:T(8,128)(2,1)S(1)}, bf16[16,512,128]{2,1,0:T(8,128)(2,1)S(1)}, bf16[16,512,128]{2,1,0:T(8,128)(2,1)S(1)}, f32[8,128]{1,0:T(8,128)S(1)}) custom-call(s32[4]{0:T(128)S(1)} %pad_add_fusion.where, f32[8,128]{1,0:T(8,128)S(1)} %copy-done.14, bf16[512,4096]{1,0:T(8,128)(2,1)S(1)} %copy-done.5, ...), custom_call_target="tpu_custom_call" | custom-call | flops 1 | bytes 17000000 | tf_op jit(solution)/shard_map/regroup/pallas_call | solution.py:244
  38.5 17.8 %all-to-all-done.got_ref = bf16[32,32,1280]{2,1,0:T(8,128)(2,1)} async-done(((bf16[32,32,1280]{2,1,0:T(8,128)(2,1)}), bf16[32,32,1280]{2,1,0:T(8,128)(2,1)}, u32[]{:S(2)}, u32[]{:S(2)}) %all-to-all-start) | async-done | bytes 2621472 | tf_op jit(solution)/shard_map/all_to_all | solution.py:627
  56.3 7.6 %attend.1 = bf16[32,32,1280]{2,1,0:T(8,128)(2,1)S(1)} custom-call(s32[16]{0:T(128)S(1)} %select_reduce_fusion.3.live, s32[64]{0:T(128)S(1)} %get-tuple-element.82.offsets, bf16[32,32,1280]{2,1,0:T(8,128)(2,1)} %all-to-all-done.got_ref, f32[512,128]{1,0:T(8,128)S(1)} %copy-done.18, f32[512,128]{1,0:T(8,128)S(1)} %copy-done.17, ...), custom_call_target="tpu_custom_call" | custom-call | flops 4000000000 | bytes 6000000 | tf_op jit(solution)/shard_map/attend/pallas_call | solution.py:332
  65.4 5.0 %all-to-all-start.1 = ((bf16[32,32,1280]{2,1,0:T(8,128)(2,1)}), bf16[32,32,1280]{2,1,0:T(8,128)(2,1)}, u32[]{:S(2)}, u32[]{:S(2)}) async-start(bf16[32,32,1280]{2,1,0:T(8,128)(2,1)} %copy-done.11), calls=%async_computation.1 | async-start | bytes 5242880 | tf_op jit(solution)/shard_map/all_to_all | solution.py:684
  71.8 3.1 %collective-permute-done.xr_hbm.xa1.b10.b11.b12.b13 = bf16[16,512,128]{2,1,0:T(8,128)(2,1)} collective-permute-done((bf16[16,512,128]{2,1,0:T(8,128)(2,1)}, bf16[16,512,128]{2,1,0:T(8,128)(2,1)}, u32[]{:S(2)}, u32[]{:S(2)}) %collective-permute-start) | collective-permute-done | bytes 2097184 | tf_op jit(solution)/shard_map/ppermute | solution.py:606
  75.0 3.0 %collective-permute-done.1.cr_hbm.c1 = bf16[16,512,128]{2,1,0:T(8,128)(2,1)} collective-permute-done((bf16[16,512,128]{2,1,0:T(8,128)(2,1)}, bf16[16,512,128]{2,1,0:T(8,128)(2,1)}, u32[]{:S(2)}, u32[]{:S(2)}) %collective-permute-start.1) | collective-permute-done | bytes 2097184 | tf_op jit(solution)/shard_map/ppermute | solution.py:606
  79.6 2.0 %collect.1 = (bf16[24,512,128]{2,1,0:T(8,128)(2,1)S(1)}, f32[8,128]{1,0:T(8,128)S(1)}) custom-call(bf16[16,512,128]{2,1,0:T(8,128)(2,1)S(1)} %get-tuple-element.47.xk_hbm.xa0.b00.b01.b02.b03, bf16[16,512,128]{2,1,0:T(8,128)(2,1)} %collective-permute-done.xr_hbm.xa1.b10.b11.b12.b13, bf16[16,512,128]{2,1,0:T(8,128)(2,1)S(1)} %copy-done.1, ...), custom_call_target="tpu_custom_call" | custom-call | flops 1 | bytes 6000000 | tf_op jit(solution)/shard_map/collect/pallas_call | solution.py:397
  81.5 1.6 copy-done.9
  83.2 21.8 %all-to-all-done.1.got_ref = bf16[32,32,1280]{2,1,0:T(8,128)(2,1)} async-done(((bf16[32,32,1280]{2,1,0:T(8,128)(2,1)}), bf16[32,32,1280]{2,1,0:T(8,128)(2,1)}, u32[]{:S(2)}, u32[]{:S(2)}) %all-to-all-start.1) | async-done | bytes 2621472 | tf_op jit(solution)/shard_map/all_to_all | solution.py:684
  104.9 2.9 %restore.1.after.dy_ref.own = bf16[512,1280]{1,0:T(8,128)(2,1)S(1)} custom-call(s32[16]{0:T(128)S(1)} %select_reduce_fusion.4.targets, bf16[32,32,1280]{2,1,0:T(8,128)(2,1)} %all-to-all-done.1.got_ref, s32[512,1]{1,0:T(8,128)S(1)} %add.100.rows_ref, f32[8,128]{1,0:T(8,128)S(1)} %get-tuple-element.51.token), custom_call_target="tpu_custom_call" | custom-call | flops 700000000 | bytes 4000000 | tf_op jit(solution)/shard_map/restore/pallas_call | solution.py:423
  109.0 2.0 %collective-permute-done.2.peer = bf16[512,1280]{1,0:T(8,128)(2,1)S(1)} collective-permute-done((bf16[512,1280]{1,0:T(8,128)(2,1)S(1)}, bf16[512,1280]{1,0:T(8,128)(2,1)S(1)}, u32[]{:S(2)}, u32[]{:S(2)}) %collective-permute-start.2) | collective-permute-done | bytes 1310752 | tf_op jit(solution)/shard_map/ppermute | solution.py:606
  113.2 3.0 %collective-permute-start.6 = (bf16[320,512]{1,0:T(8,128)(2,1)S(1)}, bf16[320,512]{1,0:T(8,128)(2,1)S(1)}, u32[]{:S(2)}, u32[]{:S(2)}) collective-permute-start(bf16[320,512]{1,0:T(8,128)(2,1)S(1)} %get-tuple-element.62), channel_id=1, source_target_pairs={{0,24},{8,0},{16,8},{24,16},{1,25},{9,1},{17,9},{25,17},{2,26},{10... | collective-permute-start | bytes 983048 | tf_op jit(solution)/shard_map/ppermute | solution.py:606
  116.2 1.7 collective-permute-start.3
  119.4 2.9 %collective-permute-done.4.refs_2_ = bf16[320,512]{1,0:T(8,128)(2,1)S(1)} collective-permute-done((bf16[320,512]{1,0:T(8,128)(2,1)S(1)}, bf16[320,512]{1,0:T(8,128)(2,1)S(1)}, u32[]{:S(2)}, u32[]{:S(2)}) %collective-permute-start.4) | collective-permute-done | bytes 327712 | tf_op jit(solution)/shard_map/ppermute | solution.py:606
  122.4 3.0 %collective-permute-start.18 = (bf16[256,1024]{1,0:T(8,128)(2,1)S(1)}, bf16[256,1024]{1,0:T(8,128)(2,1)S(1)}, u32[]{:S(2)}, u32[]{:S(2)}) collective-permute-start(bf16[256,1024]{1,0:T(8,128)(2,1)S(1)} %get-tuple-element.76), channel_id=1, source_target_pairs={{0,3},{1,0},{2,1},{3,2},{4,7},{5,4},{6,5},{7,6},{8,11},{9,8},{10,9... | collective-permute-start | bytes 1572872 | tf_op jit(solution)/shard_map/ppermute | solution.py:606
  125.4 4.6 %weight_grad.2 = (bf16[1280,512]{1,0:T(8,128)(2,1)S(1)}, bf16[1280,512]{1,0:T(8,128)(2,1)S(1)}) custom-call(bf16[320,512]{1,0:T(8,128)(2,1)S(1)} %get-tuple-element.55.after, bf16[512,1280]{1,0:T(8,128)(2,1)S(1)} %restore.1.after.dy_ref.own, bf16[512,1280]{1,0:T(8,128)(2,1)S(1)} %collective-permute-done.2.peer, ...), custom_call_target="tpu_custom_call" | custom-call | flops 2800000000 | bytes 12000000 | tf_op jit(solution)/shard_map/weight_grad/pallas_call | solution.py:517
  130.4 2.1 %input_grad.4.after.refs_0_ = bf16[1024,1024]{1,0:T(8,128)(2,1)S(1)} custom-call(bf16[1280,512]{1,0:T(8,128)(2,1)S(1)} %get-tuple-element.56.after.refs_0_, bf16[512,1280]{1,0:T(8,128)(2,1)S(1)} %restore.1.after.dy_ref.own, bf16[3072,768]{1,0:T(8,128)(2,1)S(1)} %bitcast.7), custom_call_target="tpu_custom_call" | custom-call | flops 1600000000 | bytes 10000000 | tf_op jit(solution)/shard_map/input_grad/pallas_call | solution.py:477
  132.5 3.5 %collective-permute-done.18.refs_2_ = bf16[256,1024]{1,0:T(8,128)(2,1)S(1)} collective-permute-done((bf16[256,1024]{1,0:T(8,128)(2,1)S(1)}, bf16[256,1024]{1,0:T(8,128)(2,1)S(1)}, u32[]{:S(2)}, u32[]{:S(2)}) %collective-permute-start.18) | collective-permute-done | bytes 524320 | tf_op jit(solution)/shard_map/ppermute | solution.py:606
  137.4 2.7 %collective-permute-start.20 = (bf16[512,1024]{1,0:T(8,128)(2,1)S(1)}, bf16[512,1024]{1,0:T(8,128)(2,1)S(1)}, u32[]{:S(2)}, u32[]{:S(2)}) collective-permute-start(bf16[512,1024]{1,0:T(8,128)(2,1)S(1)} %get-tuple-element.78), channel_id=1, source_target_pairs={{0,3},{1,0},{2,1},{3,2},{4,7},{5,4},{6,5},{7,6},{8,11},{9,8},{10,9... | collective-permute-start | bytes 3145736 | tf_op jit(solution)/shard_map/ppermute | solution.py:606
  142.0 5.3 %collective-permute-done.7.up_a = bf16[640,512]{1,0:T(8,128)(2,1)S(1)} collective-permute-done((bf16[640,512]{1,0:T(8,128)(2,1)S(1)}, bf16[640,512]{1,0:T(8,128)(2,1)S(1)}, u32[]{:S(2)}, u32[]{:S(2)}) %collective-permute-start.7) | collective-permute-done | bytes 655392 | tf_op jit(solution)/shard_map/ppermute | solution.py:606
  148.3 2.9 %weight_grad.3 = (bf16[640,512]{1,0:T(8,128)(2,1)S(1)}, bf16[640,512]{1,0:T(8,128)(2,1)S(1)}) custom-call(bf16[1024,1024]{1,0:T(8,128)(2,1)S(1)} %input_grad.4.after.refs_0_, bf16[512,1280]{1,0:T(8,128)(2,1)S(1)} %restore.1.after.dy_ref.own, bf16[512,1280]{1,0:T(8,128)(2,1)S(1)} %collective-permute-done.2.peer, ...), custom_call_target="tpu_custom_call" | custom-call | flops 1400000000 | bytes 6000000 | tf_op jit(solution)/shard_map/weight_grad/pallas_call | solution.py:517
  151.2 3.7 %collective-permute-done.8.down_a = bf16[640,512]{1,0:T(8,128)(2,1)S(1)} collective-permute-done((bf16[640,512]{1,0:T(8,128)(2,1)S(1)}, bf16[640,512]{1,0:T(8,128)(2,1)S(1)}, u32[]{:S(2)}, u32[]{:S(2)}) %collective-permute-start.8) | collective-permute-done | bytes 655392 | tf_op jit(solution)/shard_map/ppermute | solution.py:606
  154.9 2.5 %collective-permute-done.9.up_b = bf16[640,512]{1,0:T(8,128)(2,1)S(1)} collective-permute-done((bf16[640,512]{1,0:T(8,128)(2,1)S(1)}, bf16[640,512]{1,0:T(8,128)(2,1)S(1)}, u32[]{:S(2)}, u32[]{:S(2)}) %collective-permute-start.9) | collective-permute-done | bytes 655392 | tf_op jit(solution)/shard_map/ppermute | solution.py:606
  157.4 4.7 %collective-permute-done.10.down_b = bf16[640,512]{1,0:T(8,128)(2,1)S(1)} collective-permute-done((bf16[640,512]{1,0:T(8,128)(2,1)S(1)}, bf16[640,512]{1,0:T(8,128)(2,1)S(1)}, u32[]{:S(2)}, u32[]{:S(2)}) %collective-permute-start.10) | collective-permute-done | bytes 655392 | tf_op jit(solution)/shard_map/ppermute | solution.py:606
  163.5 2.3 %collective-permute-start.12 = (bf16[640,128]{1,0:T(8,128)(2,1)S(1)}, bf16[640,128]{1,0:T(8,128)(2,1)S(1)}, u32[]{:S(2)}, u32[]{:S(2)}) collective-permute-start(bf16[640,128]{1,0:T(8,128)(2,1)S(1)} %get-tuple-element.70), channel_id=1, source_target_pairs={{0,8},{8,16},{16,24},{24,0},{1,9},{9,17},{17,25},{25,1},{2,10},{10... | collective-permute-start | bytes 491528 | tf_op jit(solution)/shard_map/ppermute | solution.py:606
  167.0 1.8 %collective-permute-start.15 = (bf16[640,128]{1,0:T(8,128)(2,1)S(1)}, bf16[640,128]{1,0:T(8,128)(2,1)S(1)}, u32[]{:S(2)}, u32[]{:S(2)}) collective-permute-start(bf16[640,128]{1,0:T(8,128)(2,1)S(1)} %get-tuple-element.74), channel_id=1, source_target_pairs={{0,32},{32,64},{64,96},{96,0},{1,33},{33,65},{65,97},{97,1},{2,34}... | collective-permute-start | bytes 491528 | tf_op jit(solution)/shard_map/ppermute | solution.py:606
  171.3 2.4 %collective-permute-done.14.refs_5_ = bf16[640,128]{1,0:T(8,128)(2,1)S(1)} collective-permute-done((bf16[640,128]{1,0:T(8,128)(2,1)S(1)}, bf16[640,128]{1,0:T(8,128)(2,1)S(1)}, u32[]{:S(2)}, u32[]{:S(2)}) %collective-permute-start.14) | collective-permute-done | bytes 163872 | tf_op jit(solution)/shard_map/ppermute | solution.py:606
  175.3 1.9 %finish.1 = (bf16[512,1024]{1,0:T(8,128)(2,1)}, bf16[128,512]{1,0:T(8,128)(2,1)}, bf16[128,128]{1,0:T(8,128)(2,1)}, bf16[128,128]{1,0:T(8,128)(2,1)}, bf16[128,512]{1,0:T(8,128)(2,1)}) custom-call(f32[640,128]{1,0:T(8,128)S(1)} %get-tuple-element.68.refs_0_, bf16[640,128]{1,0:T(8,128)(2,1)S(1)} %collective-permute-done.11.refs_1_, ...), custom_call_target="tpu_custom_call" | custom-call | flops 1000000 | bytes 6000000 | tf_op jit(solution)/shard_map/finish/pallas_call | solution.py:593
  (107 shorter events, 29.7 us)
Async XLA Ops:
  13.2 8.6 %copy-start.7 = (bf16[4096,128]{1,0:T(8,128)(2,1)S(1)}, bf16[4096,128]{1,0:T(8,128)(2,1)}, u32[]{:S(2)}) copy-start(bf16[4096,128]{1,0:T(8,128)(2,1)} %wk_ref.3) | copy-start | bytes 3145732
  13.2 8.6 %copy-start.8 = (bf16[4096,128]{1,0:T(8,128)(2,1)S(1)}, bf16[4096,128]{1,0:T(8,128)(2,1)}, u32[]{:S(2)}) copy-start(bf16[4096,128]{1,0:T(8,128)(2,1)} %wv_ref.3) | copy-start | bytes 3145732
  13.2 8.6 %copy-start.14 = (f32[8,128]{1,0:T(8,128)S(1)}, f32[8,128]{1,0:T(8,128)}, u32[]{:S(2)}) copy-start(f32[8,128]{1,0:T(8,128)} %get-tuple-element.43.after) | copy-start | bytes 12292
  13.3 43.0 %all-to-all-start = ((bf16[32,32,1280]{2,1,0:T(8,128)(2,1)}), bf16[32,32,1280]{2,1,0:T(8,128)(2,1)}, u32[]{:S(2)}, u32[]{:S(2)}) async-start(bf16[32,32,1280]{2,1,0:T(8,128)(2,1)} %get-tuple-element.42), calls=%async_computation | async-start | bytes 5242880 | tf_op jit(solution)/shard_map/all_to_all | solution.py:627
  29.2 8.3 %copy-start.20 = (s32[2048]{0:T(1024)S(1)}, s32[2048]{0:T(1024)}, u32[]{:S(2)}) copy-start(s32[2048]{0:T(1024)} %piece_offset.1) | copy-start | bytes 24580
  29.2 27.1 %copy-start.17 = (f32[512,128]{1,0:T(8,128)S(1)}, f32[512,128]{1,0:T(8,128)}, u32[]{:S(2)}) copy-start(f32[512,128]{1,0:T(8,128)} %constant.40.clone.sin_table) | copy-start | bytes 786436
  29.2 27.1 %copy-start.18 = (f32[512,128]{1,0:T(8,128)S(1)}, f32[512,128]{1,0:T(8,128)}, u32[]{:S(2)}) copy-start(f32[512,128]{1,0:T(8,128)} %constant.39.clone.cos_table) | copy-start | bytes 786436
  65.4 39.5 %all-to-all-start.1 = ((bf16[32,32,1280]{2,1,0:T(8,128)(2,1)}), bf16[32,32,1280]{2,1,0:T(8,128)(2,1)}, u32[]{:S(2)}, u32[]{:S(2)}) async-start(bf16[32,32,1280]{2,1,0:T(8,128)(2,1)} %copy-done.11), calls=%async_computation.1 | async-start | bytes 5242880 | tf_op jit(solution)/shard_map/all_to_all | solution.py:684
  70.4 4.6 %collective-permute-start = (bf16[16,512,128]{2,1,0:T(8,128)(2,1)}, bf16[16,512,128]{2,1,0:T(8,128)(2,1)}, u32[]{:S(2)}, u32[]{:S(2)}) collective-permute-start(bf16[16,512,128]{2,1,0:T(8,128)(2,1)} %copy-done.16), channel_id=1, source_target_pairs={{0,4},{4,0},{1,5},{5,1},{2,6},{6,2},{3,7},{7,3},{8,12},{12,8},{9,1... | collective-permute-start | bytes 6291464 | tf_op jit(solution)/shard_map/ppermute | solution.py:606
  70.6 7.4 %collective-permute-start.1 = (bf16[16,512,128]{2,1,0:T(8,128)(2,1)}, bf16[16,512,128]{2,1,0:T(8,128)(2,1)}, u32[]{:S(2)}, u32[]{:S(2)}) collective-permute-start(bf16[16,512,128]{2,1,0:T(8,128)(2,1)} %copy-done.15), channel_id=1, source_target_pairs={{0,4},{4,0},{1,5},{5,1},{2,6},{6,2},{3,7},{7,3},{8,12},{12,8},{9,1... | collective-permute-start | bytes 6291464 | tf_op jit(solution)/shard_map/ppermute | solution.py:606
  107.9 3.1 %collective-permute-start.2 = (bf16[512,1280]{1,0:T(8,128)(2,1)S(1)}, bf16[512,1280]{1,0:T(8,128)(2,1)S(1)}, u32[]{:S(2)}, u32[]{:S(2)}) collective-permute-start(bf16[512,1280]{1,0:T(8,128)(2,1)S(1)} %restore.1.after.dy_ref.own), channel_id=1, source_target_pairs={{0,4},{4,0},{1,5},{5,1},{2,6},{6,2},{3,7},{7,3},{8,12},{12,8},{9,1... | collective-permute-start | bytes 3932168 | tf_op jit(solution)/shard_map/ppermute | solution.py:606
  111.0 14.4 %copy-start.2 = (bf16[16,512,128]{2,1,0:T(8,128)(2,1)S(1)}, bf16[16,512,128]{2,1,0:T(8,128)(2,1)}, u32[]{:S(2)}) copy-start(bf16[16,512,128]{2,1,0:T(8,128)(2,1)} %copy-done) | copy-start | bytes 6291460
  112.5 9.8 %collective-permute-start.4 = (bf16[320,512]{1,0:T(8,128)(2,1)S(1)}, bf16[320,512]{1,0:T(8,128)(2,1)S(1)}, u32[]{:S(2)}, u32[]{:S(2)}) collective-permute-start(bf16[320,512]{1,0:T(8,128)(2,1)S(1)} %get-tuple-element.59), channel_id=1, source_target_pairs={{0,96},{32,0},{64,32},{96,64},{1,97},{33,1},{65,33},{97,65},{2,98}... | collective-permute-start | bytes 983048 | tf_op jit(solution)/shard_map/ppermute | solution.py:606
  112.9 17.0 %collective-permute-start.5 = (bf16[320,512]{1,0:T(8,128)(2,1)S(1)}, bf16[320,512]{1,0:T(8,128)(2,1)S(1)}, u32[]{:S(2)}, u32[]{:S(2)}) collective-permute-start(bf16[320,512]{1,0:T(8,128)(2,1)S(1)} %get-tuple-element.61), channel_id=1, source_target_pairs={{0,8},{8,16},{16,24},{24,0},{1,9},{9,17},{17,25},{25,1},{2,10},{10... | collective-permute-start | bytes 983048 | tf_op jit(solution)/shard_map/ppermute | solution.py:606
  113.2 16.8 %collective-permute-start.6 = (bf16[320,512]{1,0:T(8,128)(2,1)S(1)}, bf16[320,512]{1,0:T(8,128)(2,1)S(1)}, u32[]{:S(2)}, u32[]{:S(2)}) collective-permute-start(bf16[320,512]{1,0:T(8,128)(2,1)S(1)} %get-tuple-element.62), channel_id=1, source_target_pairs={{0,24},{8,0},{16,8},{24,16},{1,25},{9,1},{17,9},{25,17},{2,26},{10... | collective-permute-start | bytes 983048 | tf_op jit(solution)/shard_map/ppermute | solution.py:606
  116.2 13.8 %collective-permute-start.3 = (bf16[320,512]{1,0:T(8,128)(2,1)S(1)}, bf16[320,512]{1,0:T(8,128)(2,1)S(1)}, u32[]{:S(2)}, u32[]{:S(2)}) collective-permute-start(bf16[320,512]{1,0:T(8,128)(2,1)S(1)} %get-tuple-element.55.after), channel_id=1, source_target_pairs={{0,32},{32,64},{64,96},{96,0},{1,33},{33,65},{65,97},{97,1},{2,34}... | collective-permute-start | bytes 983048 | tf_op jit(solution)/shard_map/ppermute | solution.py:606
  117.9 18.1 %collective-permute-start.17 = (bf16[256,1024]{1,0:T(8,128)(2,1)S(1)}, bf16[256,1024]{1,0:T(8,128)(2,1)S(1)}, u32[]{:S(2)}, u32[]{:S(2)}) collective-permute-start(bf16[256,1024]{1,0:T(8,128)(2,1)S(1)} %get-tuple-element.53.after), channel_id=1, source_target_pairs={{0,1},{1,2},{2,3},{3,0},{4,5},{5,6},{6,7},{7,4},{8,9},{9,10},{10,1... | collective-permute-start | bytes 1572872 | tf_op jit(solution)/shard_map/ppermute | solution.py:606
  122.4 8.0 %slice-start = ((s8[4718592]{0:T(1024)(128)(4,1)}), s8[4194304]{0:T(1024)(128)(4,1)S(1)}, s32[]{:S(2)}) async-start(s8[4718592]{0:T(1024)(128)(4,1)} %bitcast.6), calls=%async_computation.2 | async-start | bytes 8388608
  122.4 8.1 %slice-start.1 = ((s8[4718592]{0:T(1024)(128)(4,1)}), s8[524288]{0:T(1024)(128)(4,1)S(1)}, s32[]{:S(2)}) async-start(s8[4718592]{0:T(1024)(128)(4,1)} %bitcast.6), calls=%async_computation.3 | async-start | bytes 1048576
  122.4 13.6 %collective-permute-start.18 = (bf16[256,1024]{1,0:T(8,128)(2,1)S(1)}, bf16[256,1024]{1,0:T(8,128)(2,1)S(1)}, u32[]{:S(2)}, u32[]{:S(2)}) collective-permute-start(bf16[256,1024]{1,0:T(8,128)(2,1)S(1)} %get-tuple-element.76), channel_id=1, source_target_pairs={{0,3},{1,0},{2,1},{3,2},{4,7},{5,4},{6,5},{7,6},{8,11},{9,8},{10,9... | collective-permute-start | bytes 1572872 | tf_op jit(solution)/shard_map/ppermute | solution.py:606
  130.3 16.9 %collective-permute-start.7 = (bf16[640,512]{1,0:T(8,128)(2,1)S(1)}, bf16[640,512]{1,0:T(8,128)(2,1)S(1)}, u32[]{:S(2)}, u32[]{:S(2)}) collective-permute-start(bf16[640,512]{1,0:T(8,128)(2,1)S(1)} %get-tuple-element.63), channel_id=1, source_target_pairs={{0,32},{32,64},{64,96},{96,0},{1,33},{33,65},{65,97},{97,1},{2,34}... | collective-permute-start | bytes 1966088 | tf_op jit(solution)/shard_map/ppermute | solution.py:606
  136.3 30.5 %collective-permute-start.19 = (bf16[512,1024]{1,0:T(8,128)(2,1)S(1)}, bf16[512,1024]{1,0:T(8,128)(2,1)S(1)}, u32[]{:S(2)}, u32[]{:S(2)}) collective-permute-start(bf16[512,1024]{1,0:T(8,128)(2,1)S(1)} %get-tuple-element.77), channel_id=1, source_target_pairs={{0,1},{1,2},{2,3},{3,0},{4,5},{5,6},{6,7},{7,4},{8,9},{9,10},{10,1... | collective-permute-start | bytes 3145736 | tf_op jit(solution)/shard_map/ppermute | solution.py:606
  137.4 29.6 %collective-permute-start.20 = (bf16[512,1024]{1,0:T(8,128)(2,1)S(1)}, bf16[512,1024]{1,0:T(8,128)(2,1)S(1)}, u32[]{:S(2)}, u32[]{:S(2)}) collective-permute-start(bf16[512,1024]{1,0:T(8,128)(2,1)S(1)} %get-tuple-element.78), channel_id=1, source_target_pairs={{0,3},{1,0},{2,1},{3,2},{4,7},{5,4},{6,5},{7,6},{8,11},{9,8},{10,9... | collective-permute-start | bytes 3145736 | tf_op jit(solution)/shard_map/ppermute | solution.py:606
  140.1 14.8 %collective-permute-start.8 = (bf16[640,512]{1,0:T(8,128)(2,1)S(1)}, bf16[640,512]{1,0:T(8,128)(2,1)S(1)}, u32[]{:S(2)}, u32[]{:S(2)}) collective-permute-start(bf16[640,512]{1,0:T(8,128)(2,1)S(1)} %get-tuple-element.64), channel_id=1, source_target_pairs={{0,96},{32,0},{64,32},{96,64},{1,97},{33,1},{65,33},{97,65},{2,98}... | collective-permute-start | bytes 1966088 | tf_op jit(solution)/shard_map/ppermute | solution.py:606
  141.6 15.7 %collective-permute-start.9 = (bf16[640,512]{1,0:T(8,128)(2,1)S(1)}, bf16[640,512]{1,0:T(8,128)(2,1)S(1)}, u32[]{:S(2)}, u32[]{:S(2)}) collective-permute-start(bf16[640,512]{1,0:T(8,128)(2,1)S(1)} %get-tuple-element.66), channel_id=1, source_target_pairs={{0,8},{8,16},{16,24},{24,0},{1,9},{9,17},{17,25},{25,1},{2,10},{10... | collective-permute-start | bytes 1966088 | tf_op jit(solution)/shard_map/ppermute | solution.py:606
  147.2 14.8 %collective-permute-start.10 = (bf16[640,512]{1,0:T(8,128)(2,1)S(1)}, bf16[640,512]{1,0:T(8,128)(2,1)S(1)}, u32[]{:S(2)}, u32[]{:S(2)}) collective-permute-start(bf16[640,512]{1,0:T(8,128)(2,1)S(1)} %get-tuple-element.67), channel_id=1, source_target_pairs={{0,24},{8,0},{16,8},{24,16},{1,25},{9,1},{17,9},{25,17},{2,26},{10... | collective-permute-start | bytes 1966088 | tf_op jit(solution)/shard_map/ppermute | solution.py:606
  162.5 7.0 %collective-permute-start.11 = (bf16[640,128]{1,0:T(8,128)(2,1)S(1)}, bf16[640,128]{1,0:T(8,128)(2,1)S(1)}, u32[]{:S(2)}, u32[]{:S(2)}) collective-permute-start(bf16[640,128]{1,0:T(8,128)(2,1)S(1)} %get-tuple-element.69), channel_id=1, source_target_pairs={{0,16},{8,24},{16,0},{24,8},{1,17},{9,25},{17,1},{25,9},{2,18},{10... | collective-permute-start | bytes 491528 | tf_op jit(solution)/shard_map/ppermute | solution.py:606
  163.5 7.7 %collective-permute-start.12 = (bf16[640,128]{1,0:T(8,128)(2,1)S(1)}, bf16[640,128]{1,0:T(8,128)(2,1)S(1)}, u32[]{:S(2)}, u32[]{:S(2)}) collective-permute-start(bf16[640,128]{1,0:T(8,128)(2,1)S(1)} %get-tuple-element.70), channel_id=1, source_target_pairs={{0,8},{8,16},{16,24},{24,0},{1,9},{9,17},{17,25},{25,1},{2,10},{10... | collective-permute-start | bytes 491528 | tf_op jit(solution)/shard_map/ppermute | solution.py:606
  165.9 5.4 %collective-permute-start.13 = (bf16[640,128]{1,0:T(8,128)(2,1)S(1)}, bf16[640,128]{1,0:T(8,128)(2,1)S(1)}, u32[]{:S(2)}, u32[]{:S(2)}) collective-permute-start(bf16[640,128]{1,0:T(8,128)(2,1)S(1)} %get-tuple-element.71), channel_id=1, source_target_pairs={{0,24},{8,0},{16,8},{24,16},{1,25},{9,1},{17,9},{25,17},{2,26},{10... | collective-permute-start | bytes 491528 | tf_op jit(solution)/shard_map/ppermute | solution.py:606
  166.8 6.9 %collective-permute-start.14 = (bf16[640,128]{1,0:T(8,128)(2,1)S(1)}, bf16[640,128]{1,0:T(8,128)(2,1)S(1)}, u32[]{:S(2)}, u32[]{:S(2)}) collective-permute-start(bf16[640,128]{1,0:T(8,128)(2,1)S(1)} %get-tuple-element.73), channel_id=1, source_target_pairs={{0,64},{32,96},{64,0},{96,32},{1,65},{33,97},{65,1},{97,33},{2,66}... | collective-permute-start | bytes 491528 | tf_op jit(solution)/shard_map/ppermute | solution.py:606
  167.0 8.3 %collective-permute-start.15 = (bf16[640,128]{1,0:T(8,128)(2,1)S(1)}, bf16[640,128]{1,0:T(8,128)(2,1)S(1)}, u32[]{:S(2)}, u32[]{:S(2)}) collective-permute-start(bf16[640,128]{1,0:T(8,128)(2,1)S(1)} %get-tuple-element.74), channel_id=1, source_target_pairs={{0,32},{32,64},{64,96},{96,0},{1,33},{33,65},{65,97},{97,1},{2,34}... | collective-permute-start | bytes 491528 | tf_op jit(solution)/shard_map/ppermute | solution.py:606
  169.5 5.7 %collective-permute-start.16 = (bf16[640,128]{1,0:T(8,128)(2,1)S(1)}, bf16[640,128]{1,0:T(8,128)(2,1)S(1)}, u32[]{:S(2)}, u32[]{:S(2)}) collective-permute-start(bf16[640,128]{1,0:T(8,128)(2,1)S(1)} %get-tuple-element.75), channel_id=1, source_target_pairs={{0,96},{32,0},{64,32},{96,64},{1,97},{33,1},{65,33},{97,65},{2,98}... | collective-permute-start | bytes 491528 | tf_op jit(solution)/shard_map/ppermute | solution.py:606
  (15 other events, 43.9 us)
